TPU v7x, 512 devices: a whole 4x4x16 slice. The times are simulated.
512 devices in a mesh: lat: 64 (over z, x), mem: 8 (over y, core).
Axes of the slice: x: 4, y: 4, z: 16, core: 2. Of those that a mesh axis runs over, the one named last changes fastest.
Arguments:
- obs_rows: float32 [262144, 32], P(('lat', 'mem')), may hold values from -0.18 to 0.18
- obs_band: int32 [262144, 1], P(('lat', 'mem')), may hold values from 0 to 63; in each aligned block of 512 rows (0 to 511, 512 to 1023, ...) at most 32 rows name the same one
- obs_cell: int32 [262144], P(('lat', 'mem')), may hold values from 0 to 1439
- obs_top: int32 [262144], P(('lat', 'mem')), may hold values from 1 to 32
- perturb: bfloat16 [64, 1440, 1024], P('lat', None, 'mem'), may hold values from -6 to 6
- control: bfloat16 [64, 1440, 1024], P('lat', None, 'mem'), may hold values from -6 to 6
Outputs:
- gradient: float32 [64, 1440, 1024], P('lat', None, 'mem')
Inputs may be any that keep to these rules, and one draw needn't show every extreme that they name: `obs_band`: the 512 profiles of one device name one band each; no band is named by more than 32 profiles of one device. `obs_cell`: row within the band times 1440 plus the longitude column. `obs_top`: levels below this index carry the profile; the rest are unused.
All inputs are finite; a program needn't handle non-finite values.
Results may differ from a plain program's by a relative error of at most 0.0003.
Values sent between devices are 32-bit elements; how exact they have to be, the bound alone decides.
No kernel may reach another device: no remote copies, remote signals or barrier semaphores. Data moves between devices by JAX's collectives and lax.ppermute only.
A program may use at most 64 MiB of HBM per device.

v0:
```python
import jax
import jax.numpy as jnp
from jax import lax
from jax.sharding import PartitionSpec as P

CAP = 32


def kernel(count, spread, periodic):
    positions = jnp.arange(count, dtype=jnp.float32)
    distance = jnp.abs(positions[:, None] - positions[None, :])
    if periodic:
        distance = jnp.minimum(distance, count - distance)
    return jnp.exp(-0.5 * (distance / spread) ** 2)


def bucket(profiles, band_index, cell_index, top_level, capacity, band_count):
    levels = profiles.shape[1]
    level_mask = (jnp.arange(levels, dtype=jnp.int32)[None, :] < top_level[:, None]).astype(
        jnp.float32
    )
    onehot = (band_index[:, None] == jnp.arange(band_count, dtype=jnp.int32)[None, :]).astype(
        jnp.int32
    )
    earlier = jnp.cumsum(onehot, axis=0) - onehot
    slot_rank = jnp.sum(earlier * onehot, axis=1)
    target_slot = band_index * capacity + slot_rank
    send_rows = (
        jnp.zeros((band_count * capacity, levels), jnp.float32)
        .at[target_slot]
        .set(profiles * level_mask)
    )
    send_cells = jnp.full((band_count * capacity,), -1, jnp.int32).at[target_slot].set(cell_index)
    return (
        send_rows.reshape(band_count, capacity, levels),
        send_cells.reshape(band_count, capacity),
    )


def deposit(got_rows, got_cells, band_cells):
    levels = got_rows.shape[-1]
    flat_rows = got_rows.reshape(-1, levels)
    flat_cells = got_cells.reshape(-1)
    target_cell = jnp.where(flat_cells >= 0, flat_cells, 0)
    return jnp.zeros((band_cells, levels), jnp.float32).at[target_cell].add(flat_rows)


def zonal_rows(field, row_ids, all_rows):
    lon_count = field.shape[1]
    base = float(max(lon_count // 60, 4))

    def one_row(pair):
        row_field, row_id = pair
        latitude = 1.2 * (row_id.astype(jnp.float32) + 0.5) / all_rows
        lonk = kernel(lon_count, base / jnp.cos(latitude), True)
        return jnp.dot(
            lonk, row_field, precision=lax.Precision.HIGHEST, preferred_element_type=jnp.float32
        )

    return lax.map(one_row, (field, row_ids))


def local(obs_rows, obs_band, obs_cell, obs_top, perturb, control):
    band_count = lax.axis_size("lat")
    lat_dev, lon_count, columns = perturb.shape
    levels = obs_rows.shape[1]
    members = columns // levels
    band_cells = lat_dev * lon_count
    all_rows = lat_dev * band_count
    row_ids = lax.axis_index("lat") * lat_dev + jnp.arange(lat_dev, dtype=jnp.int32)
    send_rows, send_cells = bucket(obs_rows, obs_band[:, 0], obs_cell, obs_top, CAP, band_count)
    got_rows, got_cells = (
        lax.all_to_all(send_rows, "lat", split_axis=0, concat_axis=0, tiled=True),
        lax.all_to_all(send_cells, "lat", split_axis=0, concat_axis=0, tiled=True),
    )
    partial_grid = deposit(got_rows, got_cells, band_cells)
    innovation = lax.psum(partial_grid, "mem")
    innovation = innovation.reshape(lat_dev, lon_count, 1, levels)
    product = perturb.reshape(lat_dev, lon_count, members, levels).astype(jnp.float32) * innovation
    product = product.reshape(band_cells, columns)
    column_ids = jnp.arange(columns, dtype=jnp.int32)
    level_pos = (column_ids % levels).astype(jnp.float32)
    same_member = (column_ids[:, None] // levels == column_ids[None, :] // levels).astype(
        jnp.float32
    )
    vert_spread = 1.0
    block_vert = same_member * jnp.exp(
        -0.5 * (jnp.abs(level_pos[:, None] - level_pos[None, :]) / vert_spread) ** 2
    )
    vertical = jnp.dot(
        product, block_vert, precision=lax.Precision.HIGHEST, preferred_element_type=jnp.float32
    )
    vertical = vertical.reshape(lat_dev, lon_count, columns)
    latk = kernel(all_rows, 8.0 * lat_dev, False)
    pieces = vertical.reshape(lat_dev, band_count, lon_count * columns // band_count)
    smoothed = jnp.einsum(
        "rR,Rgc->rgc",
        latk,
        lax.all_to_all(pieces, "lat", split_axis=1, concat_axis=0, tiled=True),
        precision=lax.Precision.HIGHEST,
    )
    returned = lax.all_to_all(smoothed, "lat", split_axis=0, concat_axis=1, tiled=True)
    meridional = returned.reshape(lat_dev, lon_count, columns)
    zonal = zonal_rows(meridional, row_ids, all_rows)
    return control.astype(jnp.float32) + zonal


def solution(mesh):
    return jax.shard_map(
        local,
        mesh=mesh,
        in_specs=(
            P(("lat", "mem"), None),
            P(("lat", "mem"), None),
            P(("lat", "mem")),
            P(("lat", "mem")),
            P("lat", None, "mem"),
            P("lat", None, "mem"),
        ),
        out_specs=P("lat", None, "mem"),
        check_vma=False,
    )
```

profile of v0, /device:TPU:24, one launch (start us, length us, event | category | flops | bytes accessed | tf_op | source)
XLA Modules:
  0.0 288.2 jit_solution(6319717035383115655)
XLA Ops:
  6.5 0.7 fusion.26
  7.2 1.2 reduce-window.6
  8.4 0.2 slice_reduce_fusion
  8.7 0.8 fusion.25
  9.5 0.7 compare_select_fusion.2
  10.2 2.6 scatter_custom_fusion
  12.8 0.7 all_to_all.11
  13.5 18.6 %all-to-all-start = ((s32[64,1,32]{2,1,0:T(1,128)}), s32[64,1,32]{2,1,0:T(1,128)S(1)}, u32[]{:S(2)}, u32[]{:S(2)}) async-start(s32[64,1,32]{2,1,0:T(1,128)} %bitcast.6), calls=%async_computation | async-start | bytes 65536 | tf_op jit(solution)/shard_map/all_to_all | solution.py:74
  32.1 0.9 fusion.32
  32.9 0.1 copy.18
  33.0 2.0 scatter_custom_fusion.1
  35.0 0.0 copy-start
  35.0 1.2 reshape.231
  36.2 10.6 %all-to-all-done = s32[64,1,32]{2,1,0:T(1,128)S(1)} async-done(((s32[64,1,32]{2,1,0:T(1,128)}), s32[64,1,32]{2,1,0:T(1,128)S(1)}, u32[]{:S(2)}, u32[]{:S(2)}) %all-to-all-start) | async-done | bytes 8224 | tf_op jit(solution)/shard_map/all_to_all | solution.py:74
  46.8 4.6 %all-to-all-start.1 = ((f32[64,1,1024]{2,1,0:T(1,128)}), f32[64,1,1024]{2,1,0:T(1,128)S(1)}, u32[]{:S(2)}, u32[]{:S(2)}) async-start(f32[64,1,1024]{2,1,0:T(1,128)} %reshape.231), calls=%async_computation.1 | async-start | bytes 524288 | tf_op jit(solution)/shard_map/all_to_all | solution.py:73
  51.5 0.0 all-reduce.2.cloned.1.call-start
  51.5 0.0 copy-done
  51.5 0.2 copy.15
  51.7 0.6 broadcast.227
  52.3 0.8 reduce.6
  53.1 0.1 reshape.185
  53.2 20.2 %all-to-all-done.1 = f32[64,1,1024]{2,1,0:T(1,128)S(1)} async-done(((f32[64,1,1024]{2,1,0:T(1,128)}), f32[64,1,1024]{2,1,0:T(1,128)S(1)}, u32[]{:S(2)}, u32[]{:S(2)}) %all-to-all-start.1) | async-done | bytes 262176 | tf_op jit(solution)/shard_map/all_to_all | solution.py:73
  73.4 0.5 broadcast.229
  73.9 1.3 reduce.7
  75.2 0.3 reshape.232
  75.5 14.1 %scatter_custom_fusion.2 = f32[1440,32]{1,0:T(8,128)} fusion(s32[2048]{0:T(1024)S(1)} %bitcast.50, f32[2048,32]{1,0:T(8,128)S(1)} %bitcast.46, f32[]{:T(128)} %constant.94.clone.1), kind=kCustom, calls=%fused_computation.22 | custom fusion | flops 65536 | bytes 184324 | tf_op jit(solution)/shard_map/scatter-add | solution.py:45
  89.6 0.0 all-reduce.2.cloned.1.call-update
  89.6 65.7 %all-reduce.2.cloned.1.call-done = f32[1440,32]{1,0:T(8,128)} async-done(((f32[1440,32]{1,0:T(8,128)}), f32[1440,32]{1,0:T(8,128)}) %all-reduce.2.cloned.1.call-update) | async-done | bytes 184336 | tf_op jit(solution)/shard_map/psum | solution.py:77
  155.3 1.3 copy.19
  156.7 0.1 mul.54
  156.7 1.4 fusion.15
  158.2 0.9 reshape_reshape.4
  159.1 58.7 %all_to_all.32 = f32[1,64,2880]{2,0,1:T(1,128)S(1)} all-to-all(f32[1,64,2880]{2,0,1:T(1,128)S(1)} %reshape_reshape.4), channel_id=1, replica_groups=mesh['lat'=64,'mem'=8] {'lat'}, dimensions={1} | all-to-all | bytes 1474560 | tf_op jit(solution)/shard_map/all_to_all | solution.py:99
  217.8 0.8 convolution_bitcast_fusion
  218.6 1.6 copy.21
  220.2 5.8 %all-to-all-start.3 = ((f32[64,1,2880]{2,1,0:T(1,128)}), f32[64,1,2880]{2,1,0:T(1,128)S(1)}, u32[]{:S(2)}, u32[]{:S(2)}) async-start(f32[64,1,2880]{2,1,0:T(1,128)} %copy.21), calls=%async_computation.3 | async-start | bytes 1507328 | tf_op jit(solution)/shard_map/all_to_all | solution.py:102
  226.2 42.1 %all-to-all-done.3 = f32[64,1,2880]{2,1,0:T(1,128)S(1)} async-done(((f32[64,1,2880]{2,1,0:T(1,128)}), f32[64,1,2880]{2,1,0:T(1,128)S(1)}, u32[]{:S(2)}, u32[]{:S(2)}) %all-to-all-start.3) | async-done | bytes 737312 | tf_op jit(solution)/shard_map/all_to_all | solution.py:102
  268.3 1.8 reduce.2
  270.1 0.0 copy-start.1
  270.1 0.4 squeeze.9
  270.5 0.6 copy-done.1
  271.1 10.2 %fusion.12 = f32[1,1440,128]{2,1,0:T(8,128)} fusion(f32[1440,128]{1,0:T(8,128)S(1)} %squeeze.9, f32[]{:T(128)S(6)} %div.37, bf16[1,1440,128]{2,1,0:T(8,128)(2,1)S(1)} %copy-done.1), kind=kOutput, calls=%fused_computation.14 | convolution fusion | flops 3199933440 | bytes 1843204 | tf_op jit(solution)/shard_map/while/body/eval_jaxpr/dot_general | solution.py:56
  (4 shorter events, 0.1 us)
Async XLA Ops:
  13.5 33.3 %all-to-all-start = ((s32[64,1,32]{2,1,0:T(1,128)}), s32[64,1,32]{2,1,0:T(1,128)S(1)}, u32[]{:S(2)}, u32[]{:S(2)}) async-start(s32[64,1,32]{2,1,0:T(1,128)} %bitcast.6), calls=%async_computation | async-start | bytes 65536 | tf_op jit(solution)/shard_map/all_to_all | solution.py:74
  35.0 16.5 %copy-start = (bf16[1,1440,128]{2,1,0:T(8,128)(2,1)S(1)}, bf16[1,1440,128]{2,1,0:T(8,128)(2,1)}, u32[]{:S(2)}) copy-start(bf16[1,1440,128]{2,1,0:T(8,128)(2,1)} %param.10) | copy-start | bytes 1105924
  46.8 26.6 %all-to-all-start.1 = ((f32[64,1,1024]{2,1,0:T(1,128)}), f32[64,1,1024]{2,1,0:T(1,128)S(1)}, u32[]{:S(2)}, u32[]{:S(2)}) async-start(f32[64,1,1024]{2,1,0:T(1,128)} %reshape.231), calls=%async_computation.1 | async-start | bytes 524288 | tf_op jit(solution)/shard_map/all_to_all | solution.py:73
  51.5 103.8 %all-reduce.2.cloned.1.call-start = ((), (), s32[]{:S(2)}) async-start(), calls=%async_computation.4 | async-start | bytes 1474560 | tf_op jit(solution)/shard_map/psum | solution.py:77
  220.2 48.1 %all-to-all-start.3 = ((f32[64,1,2880]{2,1,0:T(1,128)}), f32[64,1,2880]{2,1,0:T(1,128)S(1)}, u32[]{:S(2)}, u32[]{:S(2)}) async-start(f32[64,1,2880]{2,1,0:T(1,128)} %copy.21), calls=%async_computation.3 | async-start | bytes 1507328 | tf_op jit(solution)/shard_map/all_to_all | solution.py:102
  270.1 1.0 copy-start.1
Sparse Core Ops, SparseCore 0:
  89.7 65.5 all-reduce.1
where the time goes:
time: 289 us; the launch traced here: 288 us
  waiting for transfers between devices  139 us (48%)
  blocking collectives  58.7 us (20%)
  starting transfers between devices  29.1 us (10%)
  other arithmetic  22.2 us (8%)
  between operations  13.7 us (5%)
  local copies, waits for them, and re-layouts  13.5 us (5%)
  matrix products  12.4 us (4%)
    psum x1, waiting for transfers between devices, local(): innovation = lax.psum(partial_grid, 'mem')  65.7 us
    all_to_all x1, blocking collectives, local(): lax.all_to_all(pieces, 'lat', split_axis=1, concat_axis=0, tiled=True)  58.7 us
    all_to_all x1, waiting for transfers between devices, local(): lax.all_to_all(smoothed, 'lat', split_axis=0, concat_axis=1, tiled=True)  42.1 us
    all_to_all x1, waiting for transfers between devices, local(): lax.all_to_all(send_rows, 'lat', split_axis=0, concat_axis=0, tiled=True)  20.2 us
    all_to_all x1, starting transfers between devices, local(): lax.all_to_all(send_cells, 'lat', split_axis=0, concat_axis=0, tiled=True)  18.6 us
    scatter-add x1, other arithmetic, deposit(): jnp.zeros((band_cells, levels), jnp.float32).at[target_cell].add(flat_rows)  14.1 us
    all_to_all x1, waiting for transfers between devices, local(): lax.all_to_all(send_cells, 'lat', split_axis=0, concat_axis=0, tiled=True)  10.6 us
    dot_general x1, matrix products, one_row(): jnp.dot(lonk, row_field, precision=lax.Precision.HIGHEST, preferred_eleme...  10.2 us
  transfers between devices with their start and end apart: 4, of which 4 were waited for; matrix products, arithmetic and copies ran while one was open for 2% of the time, Pallas kernels for 0%

commit v1 on v0

v1 whole, which is shorter than its diff:
```python
import functools

import jax
import jax.numpy as jnp
from jax import lax
from jax.experimental import pallas as pl
from jax.experimental.pallas import tpu as pltpu
from jax.sharding import PartitionSpec as P

CAP = 32
F32 = jnp.float32
BF16 = jnp.bfloat16
PARAMS = pltpu.CompilerParams(vmem_limit_bytes=48 * 1024 * 1024)


def split3(x):
    high = x.astype(BF16)
    rest = x - high.astype(F32)
    mid = rest.astype(BF16)
    low = (rest - mid.astype(F32)).astype(BF16)
    return high, mid, low


def split2(x):
    high = x.astype(BF16)
    return high, (x - high.astype(F32)).astype(BF16)


def dot(a, b, dims=((1,), (0,))):
    return lax.dot_general(a, b, (dims, ((), ())), preferred_element_type=F32)


def bucket_kernel(rows_ref, band_ref, cell_ref, top_ref, out_ref, bands):
    count, levels = rows_ref.shape
    band, cell, top = band_ref[...], cell_ref[...], top_ref[...]
    owner = (lax.broadcasted_iota(jnp.int32, (bands, count), 0) == band).astype(F32)
    owner_b = owner.astype(BF16)
    before = (
        lax.broadcasted_iota(jnp.int32, (count, count), 0)
        < lax.broadcasted_iota(jnp.int32, (count, count), 1)
    ).astype(F32).astype(BF16)
    earlier = dot(owner_b, before)
    rank = jnp.sum(earlier * owner, axis=0, keepdims=True).astype(jnp.int32)
    kept = lax.broadcasted_iota(jnp.int32, (levels, count), 0) < top
    values = jnp.where(kept, jnp.transpose(rows_ref[...]), 0.0)
    parts = split3(values)
    for slot in range(0, CAP, 4):
        total = None
        for part in parts:
            chosen = jnp.concatenate(
                [jnp.where(rank == slot + k, part.astype(F32), 0.0) for k in range(4)], axis=0
            ).astype(BF16)
            term = dot(owner_b, chosen, ((1,), (1,)))
            total = term if total is None else total + term
        out_ref[:, slot * levels : (slot + 4) * levels] = total
    cells = jnp.where(
        lax.broadcasted_iota(jnp.int32, (128, count), 0) == rank, cell.astype(F32), 0.0
    )
    high, low = split2(cells)
    out_ref[:, CAP * levels :] = dot(owner_b, high, ((1,), (1,))) + dot(
        owner_b, low, ((1,), (1,))
    )


def bucket(rows, band, cell, top, bands):
    count, levels = rows.shape
    return pl.pallas_call(
        functools.partial(bucket_kernel, bands=bands),
        out_shape=jax.ShapeDtypeStruct((bands, CAP * levels + 128), F32),
        compiler_params=PARAMS,
        name="bucket",
    )(rows, band.reshape(1, count), cell.reshape(1, count), top.reshape(1, count))


def deposit_kernel(got_ref, out_ref, levels):
    sources = got_ref.shape[0]
    groups, per_group, cells = out_ref.shape
    got = got_ref[...]
    width = 256 // sources
    acc = jnp.zeros((3 * levels, cells), F32)
    places = lax.broadcasted_iota(jnp.int32, (256, cells), 1).astype(F32)
    for first in range(0, CAP, width):
        block = jnp.transpose(got[:, first * levels : (first + width) * levels])
        values = jnp.concatenate(
            [block[k * levels : (k + 1) * levels] for k in range(width)], axis=1
        )
        parts = jnp.concatenate(split3(values), axis=0)
        base = CAP * levels + first
        where = jnp.concatenate([got[:, base + k : base + k + 1] for k in range(width)], axis=0)
        hits = jnp.where(places == where, 1.0, 0.0).astype(BF16)
        acc = acc + dot(parts, hits)
    grid = acc[:levels] + acc[levels : 2 * levels] + acc[2 * levels :]
    for group in range(groups):
        out_ref[group] = grid[group * per_group : (group + 1) * per_group]


def deposit(got, levels, groups, cells):
    return pl.pallas_call(
        functools.partial(deposit_kernel, levels=levels),
        out_shape=jax.ShapeDtypeStruct((groups, levels // groups, cells), F32),
        compiler_params=PARAMS,
        name="deposit",
    )(got)


def product_kernel(perturb_ref, innovation_ref, out_ref, levels):
    columns = perturb_ref.shape[1]
    groups, per_group, cells = innovation_ref.shape
    innovation = jnp.concatenate([innovation_ref[g] for g in range(groups)], axis=0)
    parts = jnp.concatenate(split3(innovation), axis=0)
    spread = (
        lax.broadcasted_iota(jnp.int32, (3 * levels, columns), 0) % levels
        == lax.broadcasted_iota(jnp.int32, (3 * levels, columns), 1) % levels
    ).astype(F32).astype(BF16)
    on_columns = dot(parts, spread, ((0,), (0,)))
    product = perturb_ref[...].astype(F32) * on_columns
    row = lax.broadcasted_iota(jnp.int32, (columns, columns), 0)
    column = lax.broadcasted_iota(jnp.int32, (columns, columns), 1)
    distance = (row % levels - column % levels).astype(F32)
    vert = jnp.where(row // levels == column // levels, jnp.exp(-0.5 * distance * distance), 0.0)
    vert_high, vert_low = split2(vert)
    high, low = split2(product)
    out_ref[...] = dot(high, vert_high) + (dot(low, vert_high) + dot(high, vert_low))


def product_vertical(perturb, innovation, levels):
    return pl.pallas_call(
        functools.partial(product_kernel, levels=levels),
        out_shape=jax.ShapeDtypeStruct(perturb.shape, F32),
        compiler_params=PARAMS,
        name="product_vertical",
    )(perturb, innovation)


def zonal_kernel(spread_ref, field_ref, control_ref, out_ref, twice, block):
    lon_count, columns = field_ref.shape
    high, low = split2(field_ref[...])
    both = jnp.concatenate([high, low], axis=1)
    twice[0:lon_count] = both
    twice[lon_count : 2 * lon_count] = both
    place = lax.broadcasted_iota(jnp.int32, (block, lon_count), 0)
    other = lax.broadcasted_iota(jnp.int32, (block, lon_count), 1)
    distance = jnp.abs(place - other).astype(F32)
    distance = jnp.minimum(distance, lon_count - distance) / spread_ref[0]
    lonk_high, lonk_low = split2(jnp.exp(-0.5 * distance * distance))
    for first in range(0, lon_count, block):
        window = twice[first : first + lon_count]
        wide = dot(lonk_high, window)
        narrow = dot(lonk_low, window[:, :columns])
        out_ref[first : first + block] = control_ref[first : first + block].astype(F32) + (
            wide[:, :columns] + (wide[:, columns:] + narrow)
        )


def zonal(field, control, spread):
    lon_count, columns = field.shape
    block = 288
    return pl.pallas_call(
        functools.partial(zonal_kernel, block=block),
        out_shape=jax.ShapeDtypeStruct(field.shape, F32),
        in_specs=[
            pl.BlockSpec(memory_space=pltpu.SMEM),
            pl.BlockSpec(memory_space=pltpu.VMEM),
            pl.BlockSpec(memory_space=pltpu.VMEM),
        ],
        scratch_shapes=[pltpu.VMEM((2 * lon_count, 2 * columns), BF16)],
        compiler_params=PARAMS,
        name="zonal",
    )(spread, field, control)


def local(obs_rows, obs_band, obs_cell, obs_top, perturb, control):
    bands, mem = lax.axis_size("lat"), lax.axis_size("mem")
    _, lon_count, columns = perturb.shape
    levels = obs_rows.shape[1]
    send = bucket(obs_rows, obs_band, obs_cell, obs_top, bands)
    got = lax.all_to_all(send, "lat", split_axis=0, concat_axis=0, tiled=True)
    partial_grid = deposit(got, levels, mem, lon_count)
    pieces = lax.all_to_all(partial_grid, "mem", split_axis=0, concat_axis=0, tiled=True)
    piece = jnp.sum(pieces, axis=0, keepdims=True)
    innovation = lax.all_to_all(
        jnp.broadcast_to(piece, pieces.shape), "mem", split_axis=0, concat_axis=0, tiled=True
    )
    vertical = product_vertical(perturb[0], innovation, levels)
    positions = jnp.arange(bands, dtype=F32)
    latk = jnp.exp(-0.5 * ((positions[:, None] - positions[None, :]) / 8.0) ** 2)
    columns_here = lax.all_to_all(
        vertical.reshape(bands, lon_count * columns // bands),
        "lat",
        split_axis=0,
        concat_axis=0,
        tiled=True,
    )
    smoothed = jnp.dot(latk, columns_here, precision=lax.Precision.HIGHEST)
    returned = lax.all_to_all(smoothed, "lat", split_axis=0, concat_axis=0, tiled=True)
    latitude = 1.2 * (lax.axis_index("lat").astype(F32) + 0.5) / bands
    spread = float(max(lon_count // 60, 4)) / jnp.cos(latitude)
    result = zonal(returned.reshape(lon_count, columns), control[0], spread.reshape(1))
    return result[None]


def solution(mesh):
    return jax.shard_map(
        local,
        mesh=mesh,
        in_specs=(
            P(("lat", "mem"), None),
            P(("lat", "mem"), None),
            P(("lat", "mem")),
            P(("lat", "mem")),
            P("lat", None, "mem"),
            P("lat", None, "mem"),
        ),
        out_specs=P("lat", None, "mem"),
        check_vma=False,
    )
```

time: 289 us -> 174 us (0.60)
  the two profiles are of different devices: /device:TPU:24 before, /device:TPU:2 now
where the time goes in v1:
time: 174 us; the launch traced here: 173 us
  blocking collectives  110 us (63%)
  waiting for transfers between devices  41.5 us (24%)
  Pallas kernels  7.51 us (4%)
  starting transfers between devices  5.96 us (3%)
  local copies, waits for them, and re-layouts  5.58 us (3%)
  other arithmetic  1.88 us (1%)
    all_to_all x1, blocking collectives, local(): lax.all_to_all(vertical.reshape(bands, lon_count * columns // bands), 'la...  48 us
    all_to_all x1, waiting for transfers between devices, local(): lax.all_to_all(smoothed, 'lat', split_axis=0, concat_axis=0, tiled=True)  41.5 us
    all_to_all x1, blocking collectives, local(): got = lax.all_to_all(send, 'lat', split_axis=0, concat_axis=0, tiled=True)  41.3 us
    all_to_all x1, blocking collectives, local(): lax.all_to_all(partial_grid, 'mem', split_axis=0, concat_axis=0, tiled=True)  11.1 us
    all_to_all x1, blocking collectives, local(): lax.all_to_all(jnp.broadcast_to(piece, pieces.shape), 'mem', split_axis=0...  9.36 us
    all_to_all x1, starting transfers between devices, local(): lax.all_to_all(smoothed, 'lat', split_axis=0, concat_axis=0, tiled=True)  5.96 us
    pallas_call x1, Pallas kernels, zonal(): pl.pallas_call(functools.partial(zonal_kernel, block=block), out_shape=ja...  3.75 us
  transfers between devices with their start and end apart: 1, of which 1 were waited for; matrix products, arithmetic and copies ran while one was open for 0% of the time, Pallas kernels for 0%

profile of v1, /device:TPU:2, one launch (start us, length us, event | category | flops | bytes accessed | tf_op | source)
XLA Modules:
  0.0 173.3 jit_solution(7706640202561876057)
XLA Ops:
  0.0 0.0 copy-start.4
  0.0 1.0 copy.8.rows_ref
  1.0 0.0 copy-start.3
  1.0 0.0 copy-start.2
  1.0 0.0 copy-done.4
  1.0 0.7 copy-done.3
  1.7 0.0 copy-done.2
  1.7 1.5 bucket.1
  3.2 0.3 copy.9
  3.5 41.3 %all_to_all.43 = f32[64,1,1152]{2,1,0:T(1,128)S(1)} all-to-all(f32[64,1,1152]{2,1,0:T(1,128)S(1)} %copy.9), channel_id=1, replica_groups=mesh['lat'=64,'mem'=8] {'lat'}, dimensions={0} | all-to-all | bytes 589824 | tf_op jit(solution)/shard_map/all_to_all | solution.py:177
  44.9 1.5 deposit.1
  46.5 11.1 %all_to_all.44 = f32[8,4,1440]{2,1,0:T(4,128)S(1)} all-to-all(f32[8,4,1440]{2,1,0:T(4,128)S(1)} %deposit.1), channel_id=1, replica_groups=mesh['lat'=64,'mem'=8] {'mem'}, dimensions={0} | all-to-all | bytes 368640 | tf_op jit(solution)/shard_map/all_to_all | solution.py:179
  57.6 0.0 copy-start
  57.7 9.4 %all_to_all.45.innovation_ref = f32[8,4,1440]{2,1,0:T(4,128)S(1)} all-to-all(f32[8,4,1440]{2,1,0:T(4,128)S(1)} %broadcast_in_dim.4), channel_id=1, replica_groups=mesh['lat'=64,'mem'=8] {'mem'}, dimensions={0} | all-to-all | bytes 368640 | tf_op jit(solution)/shard_map/all_to_all | solution.py:181
  67.0 0.0 copy-done
  67.0 0.7 product_vertical.1
  67.7 0.9 all_to_all.37
  68.7 48.0 %all_to_all.46 = f32[64,1,2880]{2,1,0:T(1,128)S(1)} all-to-all(f32[64,1,2880]{2,1,0:T(1,128)S(1)} %all_to_all.37), channel_id=1, replica_groups=mesh['lat'=64,'mem'=8] {'lat'}, dimensions={0} | all-to-all | bytes 1474560 | tf_op jit(solution)/shard_map/all_to_all | solution.py:187
  116.6 0.8 convolution_bitcast_fusion
  117.5 1.6 copy.11
  119.1 6.0 %all-to-all-start.4 = ((f32[64,1,2880]{2,1,0:T(1,128)}), f32[64,1,2880]{2,1,0:T(1,128)S(1)}, u32[]{:S(2)}, u32[]{:S(2)}) async-start(f32[64,1,2880]{2,1,0:T(1,128)} %copy.11), calls=%async_computation.4 | async-start | bytes 1507328 | tf_op jit(solution)/shard_map/all_to_all | solution.py:195
  125.2 41.5 %all-to-all-done.4 = f32[64,1,2880]{2,1,0:T(1,128)S(1)} async-done(((f32[64,1,2880]{2,1,0:T(1,128)}), f32[64,1,2880]{2,1,0:T(1,128)S(1)}, u32[]{:S(2)}, u32[]{:S(2)}) %all-to-all-start.4) | async-done | bytes 737312 | tf_op jit(solution)/shard_map/all_to_all | solution.py:195
  166.7 1.8 %reduce = f32[64,2880]{1,0:T(8,128)S(1)} reduce(f32[64,1,2880]{2,1,0:T(1,128)S(1)} %all-to-all-done.4, f32[]{:T(128)} %constant.24), dimensions={1}, to_apply=%all_to_all.36.reduce_sub_computation | reduce | bytes 1474564 | tf_op jit(solution)/shard_map/all_to_all | solution.py:195
  168.5 0.0 copy-start.1
  168.6 0.4 reshape.29.field_ref
  169.0 0.6 copy-done.1
  169.5 3.7 %zonal.1 = f32[1440,128]{1,0:T(8,128)} custom-call(f32[1]{0:T(128)} %bitcast.spread_ref, f32[1440,128]{1,0:T(8,128)S(1)} %reshape.29.field_ref, bf16[1440,128]{1,0:T(8,128)(2,1)S(1)} %bitcast.19), custom_call_target="tpu_custom_call" | custom-call | tf_op jit(solution)/shard_map/zonal/pallas_call | solution.py:158
  (3 shorter events, 0.1 us)
Async XLA Ops:
  0.0 1.0 copy-start.4
  1.0 0.7 copy-start.3
  1.0 0.7 copy-start.2
  57.6 9.4 %copy-start = (bf16[1,1440,128]{2,1,0:T(8,128)(2,1)S(1)}, bf16[1,1440,128]{2,1,0:T(8,128)(2,1)}, u32[]{:S(2)}) copy-start(bf16[1,1440,128]{2,1,0:T(8,128)(2,1)} %param.10) | copy-start | bytes 1105924
  119.1 47.6 %all-to-all-start.4 = ((f32[64,1,2880]{2,1,0:T(1,128)}), f32[64,1,2880]{2,1,0:T(1,128)S(1)}, u32[]{:S(2)}, u32[]{:S(2)}) async-start(f32[64,1,2880]{2,1,0:T(1,128)} %copy.11), calls=%async_computation.4 | async-start | bytes 1507328 | tf_op jit(solution)/shard_map/all_to_all | solution.py:195
  168.5 1.0 copy-start.1

commit v2 on v1

v2 whole, which is shorter than its diff:
```python
import functools

import jax
import jax.numpy as jnp
from jax import lax
from jax.experimental import pallas as pl
from jax.experimental.pallas import tpu as pltpu
from jax.sharding import PartitionSpec as P

CAP = 32
F32 = jnp.float32
BF16 = jnp.bfloat16
PARAMS = pltpu.CompilerParams(vmem_limit_bytes=48 * 1024 * 1024)


def split3(x):
    high = x.astype(BF16)
    rest = x - high.astype(F32)
    mid = rest.astype(BF16)
    low = (rest - mid.astype(F32)).astype(BF16)
    return high, mid, low


def split2(x):
    high = x.astype(BF16)
    return high, (x - high.astype(F32)).astype(BF16)


def dot(a, b, dims=((1,), (0,))):
    return lax.dot_general(a, b, (dims, ((), ())), preferred_element_type=F32)


def bucket_kernel(rows_ref, band_ref, cell_ref, top_ref, out_ref, bands):
    levels, count = rows_ref.shape
    band, cell, top = band_ref[...], cell_ref[...], top_ref[...]
    owner = (lax.broadcasted_iota(jnp.int32, (bands, count), 0) == band).astype(F32)
    owner_b = owner.astype(BF16)
    before = (
        lax.broadcasted_iota(jnp.int32, (count, count), 0)
        < lax.broadcasted_iota(jnp.int32, (count, count), 1)
    ).astype(F32).astype(BF16)
    earlier = dot(owner_b, before)
    rank = jnp.sum(earlier * owner, axis=0, keepdims=True).astype(jnp.int32)
    kept = lax.broadcasted_iota(jnp.int32, (levels, count), 0) < top
    values = jnp.where(kept, rows_ref[...], 0.0)
    parts = split3(values)
    for slot in range(0, CAP, 4):
        total = None
        for part in parts:
            chosen = jnp.concatenate(
                [jnp.where(rank == slot + k, part.astype(F32), 0.0) for k in range(4)], axis=0
            ).astype(BF16)
            term = dot(owner_b, chosen, ((1,), (1,)))
            total = term if total is None else total + term
        out_ref[:, slot * levels : (slot + 4) * levels] = total
    cells = jnp.where(
        lax.broadcasted_iota(jnp.int32, (128, count), 0) == rank, cell.astype(F32), 0.0
    )
    high, low = split2(cells)
    out_ref[:, CAP * levels :] = dot(owner_b, high, ((1,), (1,))) + dot(
        owner_b, low, ((1,), (1,))
    )


def bucket(rows, band, cell, top, bands):
    count, levels = rows.shape
    return pl.pallas_call(
        functools.partial(bucket_kernel, bands=bands),
        out_shape=jax.ShapeDtypeStruct((bands, CAP * levels + 128), F32),
        compiler_params=PARAMS,
        name="bucket",
    )(rows.T, band.reshape(1, count), cell.reshape(1, count), top.reshape(1, count))


def deposit_kernel(core_ref, got_ref, mine_ref, other_ref):
    sources = got_ref.shape[0]
    half, cells = mine_ref.shape
    levels = 2 * half
    got = got_ref[...]
    width = 256 // sources
    acc = jnp.zeros((3 * levels, cells), F32)
    places = lax.broadcasted_iota(jnp.int32, (256, cells), 1).astype(F32)
    for first in range(0, CAP, width):
        block = jnp.transpose(got[:, first * levels : (first + width) * levels])
        values = jnp.concatenate(
            [block[k * levels : (k + 1) * levels] for k in range(width)], axis=1
        )
        parts = jnp.concatenate(split3(values), axis=0)
        base = CAP * levels + first
        where = jnp.concatenate([got[:, base + k : base + k + 1] for k in range(width)], axis=0)
        hits = jnp.where(places == where, 1.0, 0.0).astype(BF16)
        acc = acc + dot(parts, hits)
    grid = acc[:levels] + acc[levels : 2 * levels] + acc[2 * levels :]
    first_core = core_ref[0] == 0
    mine_ref[...] = jnp.where(first_core, grid[:half], grid[half:])
    other_ref[...] = jnp.where(first_core, grid[half:], grid[:half])


def deposit(core, got, levels, cells):
    half = jax.ShapeDtypeStruct((levels // 2, cells), F32)
    return pl.pallas_call(
        deposit_kernel,
        out_shape=(half, half),
        in_specs=[
            pl.BlockSpec(memory_space=pltpu.SMEM),
            pl.BlockSpec(memory_space=pltpu.VMEM),
        ],
        compiler_params=PARAMS,
        name="deposit",
    )(core, got)


def product_kernel(core_ref, perturb_ref, mine_ref, other_ref, out_ref):
    cells, columns = perturb_ref.shape
    levels = 2 * mine_ref.shape[0]
    first_core = core_ref[0] == 0
    mine, other = mine_ref[...], other_ref[...]
    innovation = jnp.concatenate(
        [jnp.where(first_core, mine, other), jnp.where(first_core, other, mine)], axis=0
    )
    parts = jnp.concatenate(split3(innovation), axis=0)
    spread = (
        lax.broadcasted_iota(jnp.int32, (3 * levels, columns), 0) % levels
        == lax.broadcasted_iota(jnp.int32, (3 * levels, columns), 1) % levels
    ).astype(F32).astype(BF16)
    on_columns = dot(parts, spread, ((0,), (0,)))
    product = perturb_ref[...].astype(F32) * on_columns
    row = lax.broadcasted_iota(jnp.int32, (columns, columns), 0)
    column = lax.broadcasted_iota(jnp.int32, (columns, columns), 1)
    distance = (row % levels - column % levels).astype(F32)
    vert = jnp.where(row // levels == column // levels, jnp.exp(-0.5 * distance * distance), 0.0)
    vert_high, vert_low = split2(vert)
    high, low = split2(product)
    out_ref[:cells] = dot(high, vert_high) + (dot(low, vert_high) + dot(high, vert_low))
    out_ref[cells:] = jnp.zeros((out_ref.shape[0] - cells, columns), F32)


def product_vertical(core, perturb, mine, other, rows):
    return pl.pallas_call(
        product_kernel,
        out_shape=jax.ShapeDtypeStruct((rows, perturb.shape[1]), F32),
        in_specs=[pl.BlockSpec(memory_space=pltpu.SMEM)]
        + [pl.BlockSpec(memory_space=pltpu.VMEM)] * 3,
        compiler_params=PARAMS,
        name="product_vertical",
    )(core, perturb, mine, other)


def meridional_kernel(field_ref, out_ref, bands):
    each = field_ref.shape[0] // bands
    row = lax.broadcasted_iota(jnp.int32, (bands, bands), 0)
    column = lax.broadcasted_iota(jnp.int32, (bands, bands), 1)
    distance = (row - column).astype(F32) / 8.0
    high, low = split2(jnp.exp(-0.5 * distance * distance))
    weights = jnp.concatenate([high, high, low], axis=1)
    for place in range(each):
        rows = pl.ds(place, bands, stride=each)
        field_high, field_low = split2(field_ref[rows, :])
        out_ref[rows, :] = dot(
            weights, jnp.concatenate([field_high, field_low, field_high], axis=0)
        )


def meridional(field, bands):
    return pl.pallas_call(
        functools.partial(meridional_kernel, bands=bands),
        out_shape=jax.ShapeDtypeStruct(field.shape, F32),
        compiler_params=PARAMS,
        name="meridional",
    )(field)


def reach_kernel(spread_ref, high_ref, low_ref):
    block, lon_count = high_ref.shape
    place = lax.broadcasted_iota(jnp.int32, (block, lon_count), 0)
    other = lax.broadcasted_iota(jnp.int32, (block, lon_count), 1)
    distance = jnp.abs(place - other).astype(F32)
    distance = jnp.minimum(distance, lon_count - distance) / spread_ref[0]
    high_ref[...], low_ref[...] = split2(jnp.exp(-0.5 * distance * distance))


def reach(spread, block, lon_count):
    part = jax.ShapeDtypeStruct((block, lon_count), BF16)
    return pl.pallas_call(
        reach_kernel,
        out_shape=(part, part),
        in_specs=[pl.BlockSpec(memory_space=pltpu.SMEM)],
        compiler_params=PARAMS,
        cost_estimate=pl.CostEstimate(
            flops=20 * block * lon_count,
            transcendentals=block * lon_count,
            bytes_accessed=4 * block * lon_count,
        ),
        name="reach",
    )(spread)


def zonal_kernel(high_ref, low_ref, field_ref, control_ref, out_ref, twice):
    lon_count, columns = control_ref.shape
    block = high_ref.shape[0]
    high, low = split2(field_ref[:lon_count])
    both = jnp.concatenate([high, low], axis=1)
    twice[0:lon_count] = both
    twice[lon_count : 2 * lon_count] = both
    for first in range(0, lon_count, block):
        window = twice[first : first + lon_count]
        wide = dot(high_ref[...], window)
        narrow = dot(low_ref[...], window[:, :columns])
        out_ref[first : first + block] = control_ref[first : first + block].astype(F32) + (
            wide[:, :columns] + (wide[:, columns:] + narrow)
        )


def zonal(high, low, field, control):
    lon_count, columns = control.shape
    return pl.pallas_call(
        zonal_kernel,
        out_shape=jax.ShapeDtypeStruct(control.shape, F32),
        scratch_shapes=[pltpu.VMEM((2 * lon_count, 2 * columns), BF16)],
        compiler_params=PARAMS,
        name="zonal",
    )(high, low, field, control)


def local(obs_rows, obs_band, obs_cell, obs_top, perturb, control):
    bands, mem = lax.axis_size("lat"), lax.axis_size("mem")
    _, lon_count, columns = perturb.shape
    levels = obs_rows.shape[1]
    index = lax.axis_index("mem")
    core = (index % 2).astype(jnp.int32).reshape(1)

    def swap(x, flip):
        return lax.ppermute(x, "mem", [(m, m ^ flip) for m in range(mem)])

    send = bucket(obs_rows, obs_band, obs_cell, obs_top, bands)
    got = lax.all_to_all(send, "lat", split_axis=0, concat_axis=0, tiled=True)
    mine, other = deposit(core, got, levels, lon_count)
    mine = mine + swap(other, 1)
    mine = mine + swap(mine, 2)
    mine = mine + swap(mine, 6)
    other = swap(mine, 1)
    each = -(-lon_count // bands)
    padded = each * bands

    def transpose(field):
        pieces = field.reshape(bands, 1, each * columns)
        pieces = lax.all_to_all(pieces, "lat", split_axis=0, concat_axis=0, tiled=True)
        return pieces.reshape(padded, columns)

    vertical = product_vertical(core, perturb[0], mine, other, padded)
    smoothed = meridional(transpose(vertical), bands)
    returned = transpose(smoothed)
    latitude = 1.2 * (lax.axis_index("lat").astype(F32) + 0.5) / bands
    spread = float(max(lon_count // 60, 4)) / jnp.cos(latitude)
    high, low = reach(spread.reshape(1), lon_count // 5, lon_count)
    return zonal(high, low, returned, control[0])[None]


def solution(mesh):
    return jax.shard_map(
        local,
        mesh=mesh,
        in_specs=(
            P(("lat", "mem"), None),
            P(("lat", "mem"), None),
            P(("lat", "mem")),
            P(("lat", "mem")),
            P("lat", None, "mem"),
            P("lat", None, "mem"),
        ),
        out_specs=P("lat", None, "mem"),
        check_vma=False,
    )
```

time: 174 us -> 171 us (0.983)
  the two profiles are of different devices: /device:TPU:2 before, /device:TPU:24 now
where the time goes in v2:
time: 171 us
  waiting for transfers between devices  76.9 us (45%)
  blocking collectives  48.1 us (28%)
  starting transfers between devices  33.2 us (19%)
  Pallas kernels  9.44 us (6%)
  local copies, waits for them, and re-layouts  2.61 us (2%)
    all_to_all x1, blocking collectives, transpose(): lax.all_to_all(pieces, 'lat', split_axis=0, concat_axis=0, tiled=True)  48.1 us
    all_to_all x1, waiting for transfers between devices, transpose(): lax.all_to_all(pieces, 'lat', split_axis=0, concat_axis=0, tiled=True)  41.3 us
    all_to_all x1, waiting for transfers between devices, local(): got = lax.all_to_all(send, 'lat', split_axis=0, concat_axis=0, tiled=True)  23.5 us
    all_to_all x1, starting transfers between devices, local(): got = lax.all_to_all(send, 'lat', split_axis=0, concat_axis=0, tiled=True)  18.6 us
    ppermute x4, waiting for transfers between devices, swap(): return lax.ppermute(x, 'mem', [(m, m ^ flip) for m in range(mem)])  12.2 us
    ppermute x4, starting transfers between devices, swap(): return lax.ppermute(x, 'mem', [(m, m ^ flip) for m in range(mem)])  8.77 us
    all_to_all x1, starting transfers between devices, transpose(): lax.all_to_all(pieces, 'lat', split_axis=0, concat_axis=0, tiled=True)  5.83 us
  transfers between devices with their start and end apart: 6, of which 6 were waited for; matrix products, arithmetic and copies ran while one was open for 0% of the time, Pallas kernels for 1%

profile of v2, /device:TPU:24, one launch (start us, length us, event | category | flops | bytes accessed | tf_op | source)
XLA Modules:
  0.0 170.6 jit_solution(15391383998745074071)
XLA Ops:
  0.0 0.0 copy-start.5
  0.0 0.0 copy-start.4
  0.0 0.0 copy-start.3
  0.0 0.7 copy-done.5
  0.7 0.0 copy-done.4
  0.7 0.0 copy-done.3
  0.7 0.0 copy-start.2
  0.7 0.8 copy-done.2
  1.6 1.5 bucket.1
  3.1 1.0 copy.7
  4.1 18.6 %all-to-all-start = ((f32[64,1,1152]{2,1,0:T(1,128)}), f32[64,1,1152]{2,1,0:T(1,128)S(1)}, u32[]{:S(2)}, u32[]{:S(2)}) async-start(f32[64,1,1152]{2,1,0:T(1,128)} %copy.7), calls=%async_computation | async-start | bytes 589824 | tf_op jit(solution)/shard_map/all_to_all | solution.py:236
  22.7 23.5 %all-to-all-done = f32[64,1,1152]{2,1,0:T(1,128)S(1)} async-done(((f32[64,1,1152]{2,1,0:T(1,128)}), f32[64,1,1152]{2,1,0:T(1,128)S(1)}, u32[]{:S(2)}, u32[]{:S(2)}) %all-to-all-start) | async-done | bytes 294944 | tf_op jit(solution)/shard_map/all_to_all | solution.py:236
  46.2 1.5 deposit.1
  47.8 1.9 %collective-permute-start = (f32[16,1440]{1,0:T(8,128)S(1)}, f32[16,1440]{1,0:T(8,128)S(1)}, u32[]{:S(2)}, u32[]{:S(2)}) collective-permute-start(f32[16,1440]{1,0:T(8,128)S(1)} %get-tuple-element.12), channel_id=1, source_target_pairs={{0,1},{1,0},{2,3},{3,2},{4,5},{5,4},{6,7},{7,6},{8,9},{9,8},{10,11... | collective-permute-start | bytes 276488 | tf_op jit(solution)/shard_map/ppermute | solution.py:233
  49.7 1.3 collective-permute-done
  51.0 0.0 copy-start.1
  51.0 2.8 %collective-permute-start.1 = (f32[16,1440]{1,0:T(8,128)S(1)}, f32[16,1440]{1,0:T(8,128)S(1)}, u32[]{:S(2)}, u32[]{:S(2)}) collective-permute-start(f32[16,1440]{1,0:T(8,128)S(1)} %add.18), channel_id=1, source_target_pairs={{0,2},{1,3},{2,0},{3,1},{4,6},{5,7},{6,4},{7,5},{8,10},{9,11},{10,... | collective-permute-start | bytes 276488 | tf_op jit(solution)/shard_map/ppermute | solution.py:233
  53.8 4.1 %collective-permute-done.1 = f32[16,1440]{1,0:T(8,128)S(1)} collective-permute-done((f32[16,1440]{1,0:T(8,128)S(1)}, f32[16,1440]{1,0:T(8,128)S(1)}, u32[]{:S(2)}, u32[]{:S(2)}) %collective-permute-start.1) | collective-permute-done | bytes 92192 | tf_op jit(solution)/shard_map/ppermute | solution.py:233
  57.9 2.1 %collective-permute-start.2 = (f32[16,1440]{1,0:T(8,128)S(1)}, f32[16,1440]{1,0:T(8,128)S(1)}, u32[]{:S(2)}, u32[]{:S(2)}) collective-permute-start(f32[16,1440]{1,0:T(8,128)S(1)} %add.19), channel_id=1, source_target_pairs={{0,6},{1,7},{2,4},{3,5},{4,2},{5,3},{6,0},{7,1},{8,14},{9,15},{10,... | collective-permute-start | bytes 276488 | tf_op jit(solution)/shard_map/ppermute | solution.py:233
  60.0 5.6 %collective-permute-done.2 = f32[16,1440]{1,0:T(8,128)S(1)} collective-permute-done((f32[16,1440]{1,0:T(8,128)S(1)}, f32[16,1440]{1,0:T(8,128)S(1)}, u32[]{:S(2)}, u32[]{:S(2)}) %collective-permute-start.2) | collective-permute-done | bytes 92192 | tf_op jit(solution)/shard_map/ppermute | solution.py:233
  65.6 1.9 %collective-permute-start.3 = (f32[16,1440]{1,0:T(8,128)S(1)}, f32[16,1440]{1,0:T(8,128)S(1)}, u32[]{:S(2)}, u32[]{:S(2)}) collective-permute-start(f32[16,1440]{1,0:T(8,128)S(1)} %add.20.mine_ref), channel_id=1, source_target_pairs={{0,1},{1,0},{2,3},{3,2},{4,5},{5,4},{6,7},{7,6},{8,9},{9,8},{10,11... | collective-permute-start | bytes 276488 | tf_op jit(solution)/shard_map/ppermute | solution.py:233
  67.6 1.3 collective-permute-done.3.other_ref
  68.8 0.0 copy-done.1
  68.8 0.7 product_vertical.1
  69.5 48.1 %all_to_all.21 = f32[64,1,2944]{2,1,0:T(1,128)S(1)} all-to-all(f32[64,1,2944]{2,1,0:T(1,128)S(1)} %bitcast.18), channel_id=1, replica_groups=mesh['lat'=64,'mem'=8] {'lat'}, dimensions={0} | all-to-all | bytes 1507328 | tf_op jit(solution)/shard_map/all_to_all | solution.py:247
  117.6 1.5 meridional.1
  119.1 5.8 %all-to-all-start.2 = ((f32[64,1,2944]{2,1,0:T(1,128)}), f32[64,1,2944]{2,1,0:T(1,128)S(1)}, u32[]{:S(2)}, u32[]{:S(2)}) async-start(f32[64,1,2944]{2,1,0:T(1,128)} %bitcast.10), calls=%async_computation.2 | async-start | bytes 1507328 | tf_op jit(solution)/shard_map/all_to_all | solution.py:247
  125.1 0.0 copy-start
  125.1 0.9 reach.1
  126.0 41.3 %all-to-all-done.2 = f32[64,1,2944]{2,1,0:T(1,128)S(1)} async-done(((f32[64,1,2944]{2,1,0:T(1,128)}), f32[64,1,2944]{2,1,0:T(1,128)S(1)}, u32[]{:S(2)}, u32[]{:S(2)}) %all-to-all-start.2) | async-done | bytes 753696 | tf_op jit(solution)/shard_map/all_to_all | solution.py:247
  167.2 0.0 copy-done
  167.2 3.3 %zonal.1 = f32[1440,128]{1,0:T(8,128)} custom-call(bf16[288,1440]{1,0:T(8,128)(2,1)S(1)} %get-tuple-element.9.high_ref, bf16[288,1440]{1,0:T(8,128)(2,1)S(1)} %get-tuple-element.10.low_ref, f32[1472,128]{1,0:T(8,128)S(1)} %bitcast.17, bf16[1440,128]{1,0:T(8,128)(2,1)S(1)} %bitcast.22), custom_call_target="tpu_custom_call" | custom-call | tf_op jit(solution)/shard_map/zonal/pallas_call | solution.py:216
  (4 shorter events, 0.1 us)
Async XLA Ops:
  0.0 0.7 copy-start.5
  0.0 0.7 copy-start.4
  0.0 0.7 copy-start.3
  0.7 0.8 copy-start.2
  4.1 42.0 %all-to-all-start = ((f32[64,1,1152]{2,1,0:T(1,128)}), f32[64,1,1152]{2,1,0:T(1,128)S(1)}, u32[]{:S(2)}, u32[]{:S(2)}) async-start(f32[64,1,1152]{2,1,0:T(1,128)} %copy.7), calls=%async_computation | async-start | bytes 589824 | tf_op jit(solution)/shard_map/all_to_all | solution.py:236
  47.8 3.2 %collective-permute-start = (f32[16,1440]{1,0:T(8,128)S(1)}, f32[16,1440]{1,0:T(8,128)S(1)}, u32[]{:S(2)}, u32[]{:S(2)}) collective-permute-start(f32[16,1440]{1,0:T(8,128)S(1)} %get-tuple-element.12), channel_id=1, source_target_pairs={{0,1},{1,0},{2,3},{3,2},{4,5},{5,4},{6,7},{7,6},{8,9},{9,8},{10,11... | collective-permute-start | bytes 276488 | tf_op jit(solution)/shard_map/ppermute | solution.py:233
  51.0 17.8 %copy-start.1 = (bf16[1,1440,128]{2,1,0:T(8,128)(2,1)S(1)}, bf16[1,1440,128]{2,1,0:T(8,128)(2,1)}, u32[]{:S(2)}) copy-start(bf16[1,1440,128]{2,1,0:T(8,128)(2,1)} %param.10) | copy-start | bytes 1105924
  51.0 6.9 %collective-permute-start.1 = (f32[16,1440]{1,0:T(8,128)S(1)}, f32[16,1440]{1,0:T(8,128)S(1)}, u32[]{:S(2)}, u32[]{:S(2)}) collective-permute-start(f32[16,1440]{1,0:T(8,128)S(1)} %add.18), channel_id=1, source_target_pairs={{0,2},{1,3},{2,0},{3,1},{4,6},{5,7},{6,4},{7,5},{8,10},{9,11},{10,... | collective-permute-start | bytes 276488 | tf_op jit(solution)/shard_map/ppermute | solution.py:233
  57.9 7.7 %collective-permute-start.2 = (f32[16,1440]{1,0:T(8,128)S(1)}, f32[16,1440]{1,0:T(8,128)S(1)}, u32[]{:S(2)}, u32[]{:S(2)}) collective-permute-start(f32[16,1440]{1,0:T(8,128)S(1)} %add.19), channel_id=1, source_target_pairs={{0,6},{1,7},{2,4},{3,5},{4,2},{5,3},{6,0},{7,1},{8,14},{9,15},{10,... | collective-permute-start | bytes 276488 | tf_op jit(solution)/shard_map/ppermute | solution.py:233
  65.6 3.2 %collective-permute-start.3 = (f32[16,1440]{1,0:T(8,128)S(1)}, f32[16,1440]{1,0:T(8,128)S(1)}, u32[]{:S(2)}, u32[]{:S(2)}) collective-permute-start(f32[16,1440]{1,0:T(8,128)S(1)} %add.20.mine_ref), channel_id=1, source_target_pairs={{0,1},{1,0},{2,3},{3,2},{4,5},{5,4},{6,7},{7,6},{8,9},{9,8},{10,11... | collective-permute-start | bytes 276488 | tf_op jit(solution)/shard_map/ppermute | solution.py:233
  119.1 48.1 %all-to-all-start.2 = ((f32[64,1,2944]{2,1,0:T(1,128)}), f32[64,1,2944]{2,1,0:T(1,128)S(1)}, u32[]{:S(2)}, u32[]{:S(2)}) async-start(f32[64,1,2944]{2,1,0:T(1,128)} %bitcast.10), calls=%async_computation.2 | async-start | bytes 1507328 | tf_op jit(solution)/shard_map/all_to_all | solution.py:247
  125.1 42.2 %copy-start = (bf16[1,1440,128]{2,1,0:T(8,128)(2,1)S(1)}, bf16[1,1440,128]{2,1,0:T(8,128)(2,1)}, u32[]{:S(2)}) copy-start(bf16[1,1440,128]{2,1,0:T(8,128)(2,1)} %param.11) | copy-start | bytes 1105924

commit v3 on v2

v3 whole, which is shorter than its diff:
```python
import functools

import jax
import jax.numpy as jnp
from jax import lax
from jax.experimental import pallas as pl
from jax.experimental.pallas import tpu as pltpu
from jax.sharding import Mesh, PartitionSpec as P

CAP = 32
F32 = jnp.float32
BF16 = jnp.bfloat16
PARAMS = pltpu.CompilerParams(vmem_limit_bytes=20 * 1024 * 1024)


def split3(x):
    high = x.astype(BF16)
    rest = x - high.astype(F32)
    mid = rest.astype(BF16)
    low = (rest - mid.astype(F32)).astype(BF16)
    return high, mid, low


def split2(x):
    high = x.astype(BF16)
    return high, (x - high.astype(F32)).astype(BF16)


def dot(a, b, dims=((1,), (0,))):
    return lax.dot_general(a, b, (dims, ((), ())), preferred_element_type=F32)


def bucket_kernel(
    rows_any, band_any, cell_any, top_any, out_ref, rows_ref, band_ref, cell_ref, top_ref, sems
):
    levels, count = rows_ref.shape
    bands = out_ref.shape[0] * out_ref.shape[1] // (CAP * levels + 128)
    stride = out_ref.shape[0] // bands
    copies = [
        pltpu.make_async_copy(source, target, sems.at[k])
        for k, (source, target) in enumerate(
            [
                (band_any, band_ref),
                (cell_any, cell_ref),
                (top_any, top_ref),
                (rows_any, rows_ref),
            ]
        )
    ]
    for copy in copies:
        copy.start()
    before = (
        lax.broadcasted_iota(jnp.int32, (count, count), 0)
        < lax.broadcasted_iota(jnp.int32, (count, count), 1)
    ).astype(F32).astype(BF16)
    copies[0].wait()
    owner = (lax.broadcasted_iota(jnp.int32, (bands, count), 0) == band_ref[...]).astype(F32)
    owner_b = owner.astype(BF16)
    earlier = dot(owner_b, before)
    rank = jnp.sum(earlier * owner, axis=0, keepdims=True).astype(jnp.int32)
    for copy in copies[1:]:
        copy.wait()
    kept = lax.broadcasted_iota(jnp.int32, (levels, count), 0) < top_ref[...]
    parts = [part.astype(F32) for part in split3(jnp.where(kept, rows_ref[...], 0.0))]
    for place in range(stride - 1):
        total = None
        for part in parts:
            chosen = jnp.concatenate(
                [jnp.where(rank == 4 * place + k, part, 0.0) for k in range(4)], axis=0
            ).astype(BF16)
            term = dot(owner_b, chosen, ((1,), (1,)))
            total = term if total is None else total + term
        out_ref[pl.ds(place, bands, stride=stride), :] = total
    cells = jnp.where(
        lax.broadcasted_iota(jnp.int32, (128, count), 0) == rank, cell_ref[...].astype(F32), 0.0
    )
    high, low = split2(cells)
    out_ref[pl.ds(stride - 1, bands, stride=stride), :] = dot(
        owner_b, high, ((1,), (1,))
    ) + dot(owner_b, low, ((1,), (1,)))


def bucket(rows, band, cell, top, bands):
    count, levels = rows.shape
    row = pltpu.VMEM((1, count), jnp.int32)
    return pl.pallas_call(
        bucket_kernel,
        out_shape=jax.ShapeDtypeStruct((bands * (CAP * levels // 128 + 1), 128), F32),
        in_specs=[pl.BlockSpec(memory_space=pltpu.HBM)] * 4,
        scratch_shapes=[
            pltpu.VMEM((levels, count), F32),
            row,
            row,
            row,
            pltpu.SemaphoreType.DMA((4,)),
        ],
        compiler_params=PARAMS,
        name="bucket",
    )(
        *(
            pltpu.with_memory_space_constraint(x, pltpu.HBM)
            for x in (
                rows.T,
                band.reshape(1, count),
                cell.reshape(1, count),
                top.reshape(1, count),
            )
        )
    )


def deposit_kernel(got_ref, out_ref, levels):
    groups, per_group, cells = out_ref.shape
    width = 128 // levels
    stride = CAP // width + 1
    sources = got_ref.shape[0] // stride
    spots = got_ref[pl.ds(stride - 1, sources, stride=stride), :]
    acc = jnp.zeros((3 * levels, cells), F32)
    places = lax.broadcasted_iota(jnp.int32, (width * sources, cells), 1).astype(F32)
    for place in range(stride - 1):
        block = jnp.transpose(got_ref[pl.ds(place, sources, stride=stride), :])
        values = jnp.concatenate(
            [block[k * levels : (k + 1) * levels] for k in range(width)], axis=1
        )
        parts = jnp.concatenate(split3(values), axis=0)
        base = place * width
        where = jnp.concatenate([spots[:, base + k : base + k + 1] for k in range(width)], axis=0)
        hits = jnp.where(places == where, 1.0, 0.0).astype(BF16)
        acc = acc + dot(parts, hits)
    grid = acc[:levels] + acc[levels : 2 * levels] + acc[2 * levels :]
    for group in range(groups):
        out_ref[group] = grid[group * per_group : (group + 1) * per_group]


def deposit(got, levels, groups, cells):
    return pl.pallas_call(
        functools.partial(deposit_kernel, levels=levels),
        out_shape=jax.ShapeDtypeStruct((groups, levels // groups, cells), F32),
        compiler_params=PARAMS,
        name="deposit",
    )(got)


def product_kernel(perturb_ref, innovation_ref, out_ref):
    cells, columns = perturb_ref.shape
    groups, per_group, _ = innovation_ref.shape
    levels = groups * per_group
    innovation = jnp.concatenate([innovation_ref[g] for g in range(groups)], axis=0)
    parts = jnp.concatenate(split3(innovation), axis=0)
    spread = (
        lax.broadcasted_iota(jnp.int32, (3 * levels, columns), 0) % levels
        == lax.broadcasted_iota(jnp.int32, (3 * levels, columns), 1) % levels
    ).astype(F32).astype(BF16)
    on_columns = dot(parts, spread, ((0,), (0,)))
    product = perturb_ref[...].astype(F32) * on_columns
    row = lax.broadcasted_iota(jnp.int32, (columns, columns), 0)
    column = lax.broadcasted_iota(jnp.int32, (columns, columns), 1)
    distance = (row % levels - column % levels).astype(F32)
    vert = jnp.where(row // levels == column // levels, jnp.exp(-0.5 * distance * distance), 0.0)
    vert_high, vert_low = split2(vert)
    high, low = split2(product)
    out_ref[:cells] = dot(high, vert_high) + (dot(low, vert_high) + dot(high, vert_low))
    out_ref[cells:] = jnp.zeros((out_ref.shape[0] - cells, columns), F32)


def product_vertical(perturb, innovation, rows):
    return pl.pallas_call(
        product_kernel,
        out_shape=jax.ShapeDtypeStruct((rows, perturb.shape[1]), F32),
        compiler_params=PARAMS,
        name="product_vertical",
    )(perturb, innovation)


def meridional_kernel(field_ref, out_ref, bands):
    each = field_ref.shape[0] // bands
    row = lax.broadcasted_iota(jnp.int32, (bands, bands), 0)
    column = lax.broadcasted_iota(jnp.int32, (bands, bands), 1)
    distance = (row - column).astype(F32) / 8.0
    high, low = split2(jnp.exp(-0.5 * distance * distance))
    weights = jnp.concatenate([high, high, low], axis=1)
    for place in range(0, each, 2):
        places = [pl.ds(p, bands, stride=each) for p in range(place, min(place + 2, each))]
        taken = jnp.concatenate([field_ref[rows, :] for rows in places], axis=1)
        field_high, field_low = split2(taken)
        mixed = dot(weights, jnp.concatenate([field_high, field_low, field_high], axis=0))
        for k, rows in enumerate(places):
            out_ref[rows, :] = mixed[:, 128 * k : 128 * (k + 1)]


def meridional(field, bands):
    return pl.pallas_call(
        functools.partial(meridional_kernel, bands=bands),
        out_shape=jax.ShapeDtypeStruct(field.shape, F32),
        compiler_params=PARAMS,
        name="meridional",
    )(field)


def reach_kernel(spread_ref, high_ref, low_ref):
    block, lon_count = high_ref.shape
    place = lax.broadcasted_iota(jnp.int32, (block, lon_count), 0)
    other = lax.broadcasted_iota(jnp.int32, (block, lon_count), 1)
    distance = jnp.abs(place - other).astype(F32)
    distance = jnp.minimum(distance, lon_count - distance) / spread_ref[0]
    high_ref[...], low_ref[...] = split2(jnp.exp(-0.5 * distance * distance))


def reach(spread, block, lon_count):
    part = jax.ShapeDtypeStruct((block, lon_count), BF16)
    return pl.pallas_call(
        reach_kernel,
        out_shape=(part, part),
        in_specs=[pl.BlockSpec(memory_space=pltpu.SMEM)],
        compiler_params=PARAMS,
        cost_estimate=pl.CostEstimate(
            flops=20 * block * lon_count,
            transcendentals=block * lon_count,
            bytes_accessed=4 * block * lon_count,
        ),
        name="reach",
    )(spread)


def zonal_kernel(high_ref, low_ref, field_ref, control_ref, out_ref, twice):
    lon_count, columns = control_ref.shape
    block = high_ref.shape[0]
    high, low = split2(field_ref[:lon_count])
    both = jnp.concatenate([high, low], axis=1)
    twice[0:lon_count] = both
    twice[lon_count : 2 * lon_count] = both
    for first in range(0, lon_count, block):
        window = twice[first : first + lon_count]
        wide = dot(high_ref[...], window)
        narrow = dot(low_ref[...], window[:, :columns])
        out_ref[first : first + block] = control_ref[first : first + block].astype(F32) + (
            wide[:, :columns] + (wide[:, columns:] + narrow)
        )


def zonal(high, low, field, control):
    lon_count, columns = control.shape
    return pl.pallas_call(
        zonal_kernel,
        out_shape=jax.ShapeDtypeStruct(control.shape, F32),
        scratch_shapes=[pltpu.VMEM((2 * lon_count, 2 * columns), BF16)],
        compiler_params=PARAMS,
        name="zonal",
    )(high, low, field, control)


def local(obs_rows, obs_band, obs_cell, obs_top, perturb, control):
    bands = lax.axis_size("lat")
    mem = lax.axis_size("core") * lax.axis_size("y")
    _, lon_count, columns = perturb.shape
    levels = obs_rows.shape[1]

    def exchange(pieces, axes):
        return lax.all_to_all(pieces, axes, split_axis=0, concat_axis=0, tiled=True)

    send = bucket(obs_rows, obs_band, obs_cell, obs_top, bands)
    got = exchange(send.reshape(bands, 1, -1), "lat").reshape(send.shape)
    pieces = exchange(deposit(got, levels, mem, lon_count), ("core", "y"))
    piece = jnp.sum(pieces, axis=0, keepdims=True)
    innovation = exchange(jnp.broadcast_to(piece, pieces.shape), ("core", "y"))
    each = -(-lon_count // bands)
    padded = each * bands

    def transpose(field):
        pieces = field.reshape(bands, 1, each * columns)
        return exchange(pieces, "lat").reshape(padded, columns)

    vertical = product_vertical(perturb[0], innovation, padded)
    smoothed = meridional(transpose(vertical), bands)
    returned = transpose(smoothed)
    latitude = 1.2 * (lax.axis_index("lat").astype(F32) + 0.5) / bands
    spread = float(max(lon_count // 60, 4)) / jnp.cos(latitude)
    high, low = reach(spread.reshape(1), lon_count // 5, lon_count)
    return zonal(high, low, returned, control[0])[None]


def solution(mesh):
    bands, mem = mesh.shape["lat"], mesh.shape["mem"]
    finer = Mesh(mesh.devices.reshape(bands, mem // 2, 2), ("lat", "y", "core"))
    everything, members = ("lat", "y", "core"), ("y", "core")
    return jax.shard_map(
        local,
        mesh=finer,
        in_specs=(
            P(everything, None),
            P(everything, None),
            P(everything),
            P(everything),
            P("lat", None, members),
            P("lat", None, members),
        ),
        out_specs=P("lat", None, members),
        check_vma=False,
    )
```

time: 171 us -> 167 us (0.977)
  the two profiles are of different devices: /device:TPU:24 before, /device:TPU:2 now
where the time goes in v3:
time: 167 us
  blocking collectives  110 us (66%)
  waiting for transfers between devices  41.2 us (25%)
  Pallas kernels  9.96 us (6%)
  starting transfers between devices  5.95 us (4%)
    all_to_all x4, blocking collectives, exchange(): return lax.all_to_all(pieces, axes, split_axis=0, concat_axis=0, tiled=True)  110 us
    all_to_all x1, waiting for transfers between devices, exchange(): return lax.all_to_all(pieces, axes, split_axis=0, concat_axis=0, tiled=True)  41.2 us
    all_to_all x1, starting transfers between devices, exchange(): return lax.all_to_all(pieces, axes, split_axis=0, concat_axis=0, tiled=True)  5.95 us
  transfers between devices with their start and end apart: 1, of which 1 were waited for; matrix products, arithmetic and copies ran while one was open for 0% of the time, Pallas kernels for 1%

profile of v3, /device:TPU:2, one launch (start us, length us, event | category | flops | bytes accessed | tf_op | source)
XLA Modules:
  0.0 167.0 jit_solution(18145511754848665304)
XLA Ops:
  0.0 2.3 %bucket.1 = f32[576,128]{1,0:T(8,128)S(1)} custom-call(f32[32,512]{1,0:T(8,128)} %bitcast.21, s32[1,512]{1,0:T(1,128)} %bitcast.22, s32[1,512]{1,0:T(1,128)} %bitcast.23, s32[1,512]{1,0:T(1,128)} %bitcast.24), custom_call_target="tpu_custom_call" | custom-call | tf_op jit(solution)/shard_map/bucket/pallas_call | solution.py:86
  2.3 41.3 %all_to_all.25 = f32[64,1,1152]{2,1,0:T(1,128)S(1)} all-to-all(f32[64,1,1152]{2,1,0:T(1,128)S(1)} %bitcast.17), channel_id=1, replica_groups=mesh['lat'=64,'y'=4,'core'=2] {'lat'}, dimensions={0} | all-to-all | bytes 589824 | tf_op jit(solution)/shard_map/all_to_all | solution.py:259
  43.6 1.5 deposit.1
  45.2 10.6 %all_to_all.26 = f32[8,4,1440]{2,1,0:T(4,128)S(1)} all-to-all(f32[8,4,1440]{2,1,0:T(4,128)S(1)} %deposit.1), channel_id=1, replica_groups=mesh['lat'=64,'y'=4,'core'=2] {'core','y'}, dimensions={0} | all-to-all | bytes 368640 | tf_op jit(solution)/shard_map/all_to_all | solution.py:259
  55.8 0.0 copy-start.1
  55.8 9.2 %all_to_all.27.innovation_ref = f32[8,4,1440]{2,1,0:T(4,128)S(1)} all-to-all(f32[8,4,1440]{2,1,0:T(4,128)S(1)} %broadcast_in_dim.4), channel_id=1, replica_groups=mesh['lat'=64,'y'=4,'core'=2] {'core','y'}, dimensions={0} | all-to-all | bytes 368640 | tf_op jit(solution)/shard_map/all_to_all | solution.py:259
  65.0 0.0 copy-done.1
  65.0 0.7 product_vertical.1
  65.7 48.5 %all_to_all.28 = f32[64,1,2944]{2,1,0:T(1,128)S(1)} all-to-all(f32[64,1,2944]{2,1,0:T(1,128)S(1)} %bitcast.15), channel_id=1, replica_groups=mesh['lat'=64,'y'=4,'core'=2] {'lat'}, dimensions={0} | all-to-all | bytes 1507328 | tf_op jit(solution)/shard_map/all_to_all | solution.py:259
  114.3 1.3 meridional.1
  115.5 6.0 %all-to-all-start.4 = ((f32[64,1,2944]{2,1,0:T(1,128)}), f32[64,1,2944]{2,1,0:T(1,128)S(1)}, u32[]{:S(2)}, u32[]{:S(2)}) async-start(f32[64,1,2944]{2,1,0:T(1,128)} %bitcast.10), calls=%async_computation.4 | async-start | bytes 1507328 | tf_op jit(solution)/shard_map/all_to_all | solution.py:259
  121.6 0.0 copy-start
  121.6 0.9 reach.1
  122.5 41.2 %all-to-all-done.4 = f32[64,1,2944]{2,1,0:T(1,128)S(1)} async-done(((f32[64,1,2944]{2,1,0:T(1,128)}), f32[64,1,2944]{2,1,0:T(1,128)S(1)}, u32[]{:S(2)}, u32[]{:S(2)}) %all-to-all-start.4) | async-done | bytes 753696 | tf_op jit(solution)/shard_map/all_to_all | solution.py:259
  163.6 0.0 copy-done
  163.6 3.3 %zonal.1 = f32[1440,128]{1,0:T(8,128)} custom-call(bf16[288,1440]{1,0:T(8,128)(2,1)S(1)} %get-tuple-element.7.high_ref, bf16[288,1440]{1,0:T(8,128)(2,1)S(1)} %get-tuple-element.8.low_ref, f32[1472,128]{1,0:T(8,128)S(1)} %bitcast.14, bf16[1440,128]{1,0:T(8,128)(2,1)S(1)} %bitcast.19), custom_call_target="tpu_custom_call" | custom-call | tf_op jit(solution)/shard_map/zonal/pallas_call | solution.py:243
  (2 shorter events, 0.1 us)
Async XLA Ops:
  55.8 9.3 %copy-start.1 = (bf16[1,1440,128]{2,1,0:T(8,128)(2,1)S(1)}, bf16[1,1440,128]{2,1,0:T(8,128)(2,1)}, u32[]{:S(2)}) copy-start(bf16[1,1440,128]{2,1,0:T(8,128)(2,1)} %param.10) | copy-start | bytes 1105924
  115.5 48.1 %all-to-all-start.4 = ((f32[64,1,2944]{2,1,0:T(1,128)}), f32[64,1,2944]{2,1,0:T(1,128)S(1)}, u32[]{:S(2)}, u32[]{:S(2)}) async-start(f32[64,1,2944]{2,1,0:T(1,128)} %bitcast.10), calls=%async_computation.4 | async-start | bytes 1507328 | tf_op jit(solution)/shard_map/all_to_all | solution.py:259
  121.6 42.0 %copy-start = (bf16[1,1440,128]{2,1,0:T(8,128)(2,1)S(1)}, bf16[1,1440,128]{2,1,0:T(8,128)(2,1)}, u32[]{:S(2)}) copy-start(bf16[1,1440,128]{2,1,0:T(8,128)(2,1)} %param.11) | copy-start | bytes 1105924

commit v4 on v3

--- a/solution.py
+++ b/solution.py
@@ -141,7 +141,8 @@
     )(got)
 
 
-def product_kernel(perturb_ref, innovation_ref, out_ref):
+def product_kernel(turn_ref, perturb_ref, innovation_ref, out_ref):
+    del turn_ref
     cells, columns = perturb_ref.shape
     groups, per_group, _ = innovation_ref.shape
     levels = groups * per_group
@@ -163,13 +164,13 @@
     out_ref[cells:] = jnp.zeros((out_ref.shape[0] - cells, columns), F32)
 
 
-def product_vertical(perturb, innovation, rows):
+def product_vertical(turn, perturb, innovation, rows):
     return pl.pallas_call(
         product_kernel,
         out_shape=jax.ShapeDtypeStruct((rows, perturb.shape[1]), F32),
         compiler_params=PARAMS,
         name="product_vertical",
-    )(perturb, innovation)
+    )(turn, perturb, innovation)
 
 
 def meridional_kernel(field_ref, out_ref, bands):
@@ -270,7 +271,12 @@
         pieces = field.reshape(bands, 1, each * columns)
         return exchange(pieces, "lat").reshape(padded, columns)
 
-    vertical = product_vertical(perturb[0], innovation, padded)
+    rings = lax.axis_size("y")
+    second = [(2 * y + 1, 2 * ((y + 1) % rings) + 1) for y in range(rings)]
+    turn = innovation[0, :, :128]
+    for _ in range(4):
+        turn = lax.ppermute(turn, ("y", "core"), second)
+    vertical = product_vertical(turn, perturb[0], innovation, padded)
     smoothed = meridional(transpose(vertical), bands)
     returned = transpose(smoothed)
     latitude = 1.2 * (lax.axis_index("lat").astype(F32) + 0.5) / bands

time: 167 us -> 159 us (0.952)
  the two profiles are of different devices: /device:TPU:2 before, /device:TPU:1 now
where the time goes in v4:
time: 159 us
  blocking collectives  94.4 us (59%)
  waiting for transfers between devices  40.2 us (25%)
  starting transfers between devices  14 us (9%)
  Pallas kernels  9.96 us (6%)
    all_to_all x4, blocking collectives, exchange(): return lax.all_to_all(pieces, axes, split_axis=0, concat_axis=0, tiled=True)  94.4 us
    all_to_all x1, waiting for transfers between devices, exchange(): return lax.all_to_all(pieces, axes, split_axis=0, concat_axis=0, tiled=True)  25.8 us
    ppermute x4, waiting for transfers between devices, local(): turn = lax.ppermute(turn, ('y', 'core'), second)  14.5 us
    ppermute x4, starting transfers between devices, local(): turn = lax.ppermute(turn, ('y', 'core'), second)  8.2 us
    all_to_all x1, starting transfers between devices, exchange(): return lax.all_to_all(pieces, axes, split_axis=0, concat_axis=0, tiled=True)  5.81 us
    pallas_call x1, Pallas kernels, zonal(): pl.pallas_call(zonal_kernel, out_shape=jax.ShapeDtypeStruct(control.shape...  3.32 us
  transfers between devices with their start and end apart: 5, of which 5 were waited for; matrix products, arithmetic and copies ran while one was open for 0% of the time, Pallas kernels for 1%

profile of v4, /device:TPU:1, one launch (start us, length us, event | category | flops | bytes accessed | tf_op | source)
XLA Modules:
  0.0 158.9 jit_solution(7817144443907158838)
XLA Ops:
  0.0 2.3 %bucket.1 = f32[576,128]{1,0:T(8,128)S(1)} custom-call(f32[32,512]{1,0:T(8,128)} %bitcast.23, s32[1,512]{1,0:T(1,128)} %bitcast.24, s32[1,512]{1,0:T(1,128)} %bitcast.25, s32[1,512]{1,0:T(1,128)} %bitcast.26), custom_call_target="tpu_custom_call" | custom-call | tf_op jit(solution)/shard_map/bucket/pallas_call | solution.py:86
  2.3 39.4 %all_to_all.25 = f32[64,1,1152]{2,1,0:T(1,128)S(1)} all-to-all(f32[64,1,1152]{2,1,0:T(1,128)S(1)} %bitcast.19), channel_id=1, replica_groups=mesh['lat'=64,'y'=4,'core'=2] {'lat'}, dimensions={0} | all-to-all | bytes 589824 | tf_op jit(solution)/shard_map/all_to_all | solution.py:260
  41.7 1.5 deposit.1
  43.2 14.2 %all_to_all.26 = f32[8,4,1440]{2,1,0:T(4,128)S(1)} all-to-all(f32[8,4,1440]{2,1,0:T(4,128)S(1)} %deposit.1), channel_id=1, replica_groups=mesh['lat'=64,'y'=4,'core'=2] {'core','y'}, dimensions={0} | all-to-all | bytes 368640 | tf_op jit(solution)/shard_map/all_to_all | solution.py:260
  57.4 0.0 copy-start.1
  57.4 9.2 %all_to_all.27.innovation_ref = f32[8,4,1440]{2,1,0:T(4,128)S(1)} all-to-all(f32[8,4,1440]{2,1,0:T(4,128)S(1)} %broadcast_in_dim.4), channel_id=1, replica_groups=mesh['lat'=64,'y'=4,'core'=2] {'core','y'}, dimensions={0} | all-to-all | bytes 368640 | tf_op jit(solution)/shard_map/all_to_all | solution.py:260
  66.6 2.5 %collective-permute-start = (f32[4,128]{1,0:T(4,128)S(1)}, f32[4,128]{1,0:T(4,128)S(1)}, u32[]{:S(2)}, u32[]{:S(2)}) collective-permute-start(f32[4,128]{1,0:T(4,128)S(1)} %slice_bitcast_fusion), channel_id=1, source_target_pairs={{1,3},{3,5},{5,7},{7,1},{9,11},{11,13},{13,15},{15,9},{17,19},{19,... | collective-permute-start | bytes 6152 | tf_op jit(solution)/shard_map/ppermute | solution.py:278
  69.1 3.0 %collective-permute-done = f32[4,128]{1,0:T(4,128)S(1)} collective-permute-done((f32[4,128]{1,0:T(4,128)S(1)}, f32[4,128]{1,0:T(4,128)S(1)}, u32[]{:S(2)}, u32[]{:S(2)}) %collective-permute-start) | collective-permute-done | bytes 2080 | tf_op jit(solution)/shard_map/ppermute | solution.py:278
  72.2 1.9 %collective-permute-start.1 = (f32[4,128]{1,0:T(4,128)S(1)}, f32[4,128]{1,0:T(4,128)S(1)}, u32[]{:S(2)}, u32[]{:S(2)}) collective-permute-start(f32[4,128]{1,0:T(4,128)S(1)} %collective-permute-done), channel_id=1, source_target_pairs={{1,3},{3,5},{5,7},{7,1},{9,11},{11,13},{13,15},{15,9},{17,19},{19,... | collective-permute-start | bytes 6152 | tf_op jit(solution)/shard_map/ppermute | solution.py:278
  74.1 3.6 %collective-permute-done.1 = f32[4,128]{1,0:T(4,128)S(1)} collective-permute-done((f32[4,128]{1,0:T(4,128)S(1)}, f32[4,128]{1,0:T(4,128)S(1)}, u32[]{:S(2)}, u32[]{:S(2)}) %collective-permute-start.1) | collective-permute-done | bytes 2080 | tf_op jit(solution)/shard_map/ppermute | solution.py:278
  77.7 1.9 %collective-permute-start.2 = (f32[4,128]{1,0:T(4,128)S(1)}, f32[4,128]{1,0:T(4,128)S(1)}, u32[]{:S(2)}, u32[]{:S(2)}) collective-permute-start(f32[4,128]{1,0:T(4,128)S(1)} %collective-permute-done.1), channel_id=1, source_target_pairs={{1,3},{3,5},{5,7},{7,1},{9,11},{11,13},{13,15},{15,9},{17,19},{19,... | collective-permute-start | bytes 6152 | tf_op jit(solution)/shard_map/ppermute | solution.py:278
  79.6 3.9 %collective-permute-done.2 = f32[4,128]{1,0:T(4,128)S(1)} collective-permute-done((f32[4,128]{1,0:T(4,128)S(1)}, f32[4,128]{1,0:T(4,128)S(1)}, u32[]{:S(2)}, u32[]{:S(2)}) %collective-permute-start.2) | collective-permute-done | bytes 2080 | tf_op jit(solution)/shard_map/ppermute | solution.py:278
  83.5 1.9 %collective-permute-start.3 = (f32[4,128]{1,0:T(4,128)S(1)}, f32[4,128]{1,0:T(4,128)S(1)}, u32[]{:S(2)}, u32[]{:S(2)}) collective-permute-start(f32[4,128]{1,0:T(4,128)S(1)} %collective-permute-done.2), channel_id=1, source_target_pairs={{1,3},{3,5},{5,7},{7,1},{9,11},{11,13},{13,15},{15,9},{17,19},{19,... | collective-permute-start | bytes 6152 | tf_op jit(solution)/shard_map/ppermute | solution.py:278
  85.4 3.9 %collective-permute-done.3.turn_ref = f32[4,128]{1,0:T(4,128)S(1)} collective-permute-done((f32[4,128]{1,0:T(4,128)S(1)}, f32[4,128]{1,0:T(4,128)S(1)}, u32[]{:S(2)}, u32[]{:S(2)}) %collective-permute-start.3) | collective-permute-done | bytes 2080 | tf_op jit(solution)/shard_map/ppermute | solution.py:278
  89.4 0.0 copy-done.1
  89.4 0.7 product_vertical.1
  90.0 31.6 %all_to_all.28 = f32[64,1,2944]{2,1,0:T(1,128)S(1)} all-to-all(f32[64,1,2944]{2,1,0:T(1,128)S(1)} %bitcast.17), channel_id=1, replica_groups=mesh['lat'=64,'y'=4,'core'=2] {'lat'}, dimensions={0} | all-to-all | bytes 1507328 | tf_op jit(solution)/shard_map/all_to_all | solution.py:260
  121.7 1.3 meridional.1
  123.0 5.8 %all-to-all-start.4 = ((f32[64,1,2944]{2,1,0:T(1,128)}), f32[64,1,2944]{2,1,0:T(1,128)S(1)}, u32[]{:S(2)}, u32[]{:S(2)}) async-start(f32[64,1,2944]{2,1,0:T(1,128)} %bitcast.11), calls=%async_computation.4 | async-start | bytes 1507328 | tf_op jit(solution)/shard_map/all_to_all | solution.py:260
  128.9 0.0 copy-start
  128.9 0.9 reach.1
  129.8 25.8 %all-to-all-done.4 = f32[64,1,2944]{2,1,0:T(1,128)S(1)} async-done(((f32[64,1,2944]{2,1,0:T(1,128)}), f32[64,1,2944]{2,1,0:T(1,128)S(1)}, u32[]{:S(2)}, u32[]{:S(2)}) %all-to-all-start.4) | async-done | bytes 753696 | tf_op jit(solution)/shard_map/all_to_all | solution.py:260
  155.5 0.0 copy-done
  155.5 3.3 %zonal.1 = f32[1440,128]{1,0:T(8,128)} custom-call(bf16[288,1440]{1,0:T(8,128)(2,1)S(1)} %get-tuple-element.7.high_ref, bf16[288,1440]{1,0:T(8,128)(2,1)S(1)} %get-tuple-element.8.low_ref, f32[1472,128]{1,0:T(8,128)S(1)} %bitcast.16, bf16[1440,128]{1,0:T(8,128)(2,1)S(1)} %bitcast.21), custom_call_target="tpu_custom_call" | custom-call | tf_op jit(solution)/shard_map/zonal/pallas_call | solution.py:244
  (3 shorter events, 0.1 us)
Async XLA Ops:
  57.4 32.0 %copy-start.1 = (bf16[1,1440,128]{2,1,0:T(8,128)(2,1)S(1)}, bf16[1,1440,128]{2,1,0:T(8,128)(2,1)}, u32[]{:S(2)}) copy-start(bf16[1,1440,128]{2,1,0:T(8,128)(2,1)} %param.10) | copy-start | bytes 1105924
  66.6 5.5 %collective-permute-start = (f32[4,128]{1,0:T(4,128)S(1)}, f32[4,128]{1,0:T(4,128)S(1)}, u32[]{:S(2)}, u32[]{:S(2)}) collective-permute-start(f32[4,128]{1,0:T(4,128)S(1)} %slice_bitcast_fusion), channel_id=1, source_target_pairs={{1,3},{3,5},{5,7},{7,1},{9,11},{11,13},{13,15},{15,9},{17,19},{19,... | collective-permute-start | bytes 6152 | tf_op jit(solution)/shard_map/ppermute | solution.py:278
  72.2 5.5 %collective-permute-start.1 = (f32[4,128]{1,0:T(4,128)S(1)}, f32[4,128]{1,0:T(4,128)S(1)}, u32[]{:S(2)}, u32[]{:S(2)}) collective-permute-start(f32[4,128]{1,0:T(4,128)S(1)} %collective-permute-done), channel_id=1, source_target_pairs={{1,3},{3,5},{5,7},{7,1},{9,11},{11,13},{13,15},{15,9},{17,19},{19,... | collective-permute-start | bytes 6152 | tf_op jit(solution)/shard_map/ppermute | solution.py:278
  77.7 5.8 %collective-permute-start.2 = (f32[4,128]{1,0:T(4,128)S(1)}, f32[4,128]{1,0:T(4,128)S(1)}, u32[]{:S(2)}, u32[]{:S(2)}) collective-permute-start(f32[4,128]{1,0:T(4,128)S(1)} %collective-permute-done.1), channel_id=1, source_target_pairs={{1,3},{3,5},{5,7},{7,1},{9,11},{11,13},{13,15},{15,9},{17,19},{19,... | collective-permute-start | bytes 6152 | tf_op jit(solution)/shard_map/ppermute | solution.py:278
  83.5 5.8 %collective-permute-start.3 = (f32[4,128]{1,0:T(4,128)S(1)}, f32[4,128]{1,0:T(4,128)S(1)}, u32[]{:S(2)}, u32[]{:S(2)}) collective-permute-start(f32[4,128]{1,0:T(4,128)S(1)} %collective-permute-done.2), channel_id=1, source_target_pairs={{1,3},{3,5},{5,7},{7,1},{9,11},{11,13},{13,15},{15,9},{17,19},{19,... | collective-permute-start | bytes 6152 | tf_op jit(solution)/shard_map/ppermute | solution.py:278
  123.0 32.6 %all-to-all-start.4 = ((f32[64,1,2944]{2,1,0:T(1,128)}), f32[64,1,2944]{2,1,0:T(1,128)S(1)}, u32[]{:S(2)}, u32[]{:S(2)}) async-start(f32[64,1,2944]{2,1,0:T(1,128)} %bitcast.11), calls=%async_computation.4 | async-start | bytes 1507328 | tf_op jit(solution)/shard_map/all_to_all | solution.py:260
  128.9 26.6 %copy-start = (bf16[1,1440,128]{2,1,0:T(8,128)(2,1)S(1)}, bf16[1,1440,128]{2,1,0:T(8,128)(2,1)}, u32[]{:S(2)}) copy-start(bf16[1,1440,128]{2,1,0:T(8,128)(2,1)} %param.11) | copy-start | bytes 1105924

commit v5 on v4

--- a/solution.py
+++ b/solution.py
@@ -230,13 +230,17 @@
     both = jnp.concatenate([high, low], axis=1)
     twice[0:lon_count] = both
     twice[lon_count : 2 * lon_count] = both
-    for first in range(0, lon_count, block):
-        window = twice[first : first + lon_count]
-        wide = dot(high_ref[...], window)
-        narrow = dot(low_ref[...], window[:, :columns])
-        out_ref[first : first + block] = control_ref[first : first + block].astype(F32) + (
-            wide[:, :columns] + (wide[:, columns:] + narrow)
-        )
+    starts = list(range(0, lon_count, block))
+    for pair in range(0, len(starts), 2):
+        windows = [twice[first : first + lon_count] for first in starts[pair : pair + 2]]
+        narrow = dot(low_ref[...], jnp.concatenate([w[:, :columns] for w in windows], axis=1))
+        for k, window in enumerate(windows):
+            wide = dot(high_ref[...], window)
+            rows = pl.ds(starts[pair + k], block)
+            out_ref[rows] = control_ref[rows].astype(F32) + (
+                wide[:, :columns]
+                + (wide[:, columns:] + narrow[:, k * columns : (k + 1) * columns])
+            )
 
 
 def zonal(high, low, field, control):
@@ -273,8 +277,8 @@
 
     rings = lax.axis_size("y")
     second = [(2 * y + 1, 2 * ((y + 1) % rings) + 1) for y in range(rings)]
-    turn = innovation[0, :, :128]
-    for _ in range(4):
+    turn = innovation[:4]
+    for _ in range(3):
         turn = lax.ppermute(turn, ("y", "core"), second)
     vertical = product_vertical(turn, perturb[0], innovation, padded)
     smoothed = meridional(transpose(vertical), bands)

time: 159 us -> 158 us (level); the launches traced: 159 us -> 156 us
  starting transfers between devices: 14 us -> 12 us
    ppermute x4 -> x3, starting transfers between devices: 8.2 us -> 6.3 us  [local(): turn = lax.ppermute(turn, ('y', 'core'), second)]
    ppermute x4 -> x3, waiting for transfers between devices: 14.5 us -> 14 us  [local(): turn = lax.ppermute(turn, ('y', 'core'), second)]
  transfers between devices with their start and end apart: 5 -> 4, of which waited for: 5 -> 4; matrix products, arithmetic and copies ran while one was open for 0% -> 0% of each run, Pallas kernels for 1% -> 1%
where the time goes in v5:
time: 158 us; the launch traced here: 156 us
  blocking collectives  94.4 us (60%)
  waiting for transfers between devices  40.1 us (25%)
  starting transfers between devices  12 us (8%)
  Pallas kernels  9.51 us (6%)
    all_to_all x4, blocking collectives, exchange(): return lax.all_to_all(pieces, axes, split_axis=0, concat_axis=0, tiled=True)  94.4 us
    all_to_all x1, waiting for transfers between devices, exchange(): return lax.all_to_all(pieces, axes, split_axis=0, concat_axis=0, tiled=True)  26.1 us
    ppermute x3, waiting for transfers between devices, local(): turn = lax.ppermute(turn, ('y', 'core'), second)  14 us
    ppermute x3, starting transfers between devices, local(): turn = lax.ppermute(turn, ('y', 'core'), second)  6.3 us
    all_to_all x1, starting transfers between devices, exchange(): return lax.all_to_all(pieces, axes, split_axis=0, concat_axis=0, tiled=True)  5.7 us
  transfers between devices with their start and end apart: 4, of which 4 were waited for; matrix products, arithmetic and copies ran while one was open for 0% of the time, Pallas kernels for 1%

profile of v5, /device:TPU:1, one launch (start us, length us, event | category | flops | bytes accessed | tf_op | source)
XLA Modules:
  0.0 156.2 jit_solution(13814913924972494416)
XLA Ops:
  0.0 2.3 %bucket.1 = f32[576,128]{1,0:T(8,128)S(1)} custom-call(f32[32,512]{1,0:T(8,128)} %bitcast.21, s32[1,512]{1,0:T(1,128)} %bitcast.22, s32[1,512]{1,0:T(1,128)} %bitcast.23, s32[1,512]{1,0:T(1,128)} %bitcast.24), custom_call_target="tpu_custom_call" | custom-call | tf_op jit(solution)/shard_map/bucket/pallas_call | solution.py:86
  2.3 39.4 %all_to_all.25 = f32[64,1,1152]{2,1,0:T(1,128)S(1)} all-to-all(f32[64,1,1152]{2,1,0:T(1,128)S(1)} %bitcast.17), channel_id=1, replica_groups=mesh['lat'=64,'y'=4,'core'=2] {'lat'}, dimensions={0} | all-to-all | bytes 589824 | tf_op jit(solution)/shard_map/all_to_all | solution.py:264
  41.7 1.5 deposit.1
  43.2 14.2 %all_to_all.26 = f32[8,4,1440]{2,1,0:T(4,128)S(1)} all-to-all(f32[8,4,1440]{2,1,0:T(4,128)S(1)} %deposit.1), channel_id=1, replica_groups=mesh['lat'=64,'y'=4,'core'=2] {'core','y'}, dimensions={0} | all-to-all | bytes 368640 | tf_op jit(solution)/shard_map/all_to_all | solution.py:264
  57.4 0.0 copy-start.1
  57.4 9.2 %all_to_all.27.innovation_ref = f32[8,4,1440]{2,1,0:T(4,128)S(1)} all-to-all(f32[8,4,1440]{2,1,0:T(4,128)S(1)} %broadcast_in_dim.4), channel_id=1, replica_groups=mesh['lat'=64,'y'=4,'core'=2] {'core','y'}, dimensions={0} | all-to-all | bytes 368640 | tf_op jit(solution)/shard_map/all_to_all | solution.py:264
  66.7 2.5 %collective-permute-start = (f32[4,4,1440]{2,1,0:T(4,128)S(1)}, f32[4,4,1440]{2,1,0:T(4,128)S(1)}, u32[]{:S(2)}, u32[]{:S(2)}) collective-permute-start(f32[4,4,1440]{2,1,0:T(4,128)S(1)} %slice.4), channel_id=1, source_target_pairs={{1,3},{3,5},{5,7},{7,1},{9,11},{11,13},{13,15},{15,9},{17,19},{19,... | collective-permute-start | bytes 276488 | tf_op jit(solution)/shard_map/ppermute | solution.py:282
  69.2 4.1 %collective-permute-done = f32[4,4,1440]{2,1,0:T(4,128)S(1)} collective-permute-done((f32[4,4,1440]{2,1,0:T(4,128)S(1)}, f32[4,4,1440]{2,1,0:T(4,128)S(1)}, u32[]{:S(2)}, u32[]{:S(2)}) %collective-permute-start) | collective-permute-done | bytes 92192 | tf_op jit(solution)/shard_map/ppermute | solution.py:282
  73.2 1.9 %collective-permute-start.1 = (f32[4,4,1440]{2,1,0:T(4,128)S(1)}, f32[4,4,1440]{2,1,0:T(4,128)S(1)}, u32[]{:S(2)}, u32[]{:S(2)}) collective-permute-start(f32[4,4,1440]{2,1,0:T(4,128)S(1)} %collective-permute-done), channel_id=1, source_target_pairs={{1,3},{3,5},{5,7},{7,1},{9,11},{11,13},{13,15},{15,9},{17,19},{19,... | collective-permute-start | bytes 276488 | tf_op jit(solution)/shard_map/ppermute | solution.py:282
  75.2 4.9 %collective-permute-done.1 = f32[4,4,1440]{2,1,0:T(4,128)S(1)} collective-permute-done((f32[4,4,1440]{2,1,0:T(4,128)S(1)}, f32[4,4,1440]{2,1,0:T(4,128)S(1)}, u32[]{:S(2)}, u32[]{:S(2)}) %collective-permute-start.1) | collective-permute-done | bytes 92192 | tf_op jit(solution)/shard_map/ppermute | solution.py:282
  80.1 1.9 %collective-permute-start.2 = (f32[4,4,1440]{2,1,0:T(4,128)S(1)}, f32[4,4,1440]{2,1,0:T(4,128)S(1)}, u32[]{:S(2)}, u32[]{:S(2)}) collective-permute-start(f32[4,4,1440]{2,1,0:T(4,128)S(1)} %collective-permute-done.1), channel_id=1, source_target_pairs={{1,3},{3,5},{5,7},{7,1},{9,11},{11,13},{13,15},{15,9},{17,19},{19,... | collective-permute-start | bytes 276488 | tf_op jit(solution)/shard_map/ppermute | solution.py:282
  82.0 4.9 %collective-permute-done.2.turn_ref = f32[4,4,1440]{2,1,0:T(4,128)S(1)} collective-permute-done((f32[4,4,1440]{2,1,0:T(4,128)S(1)}, f32[4,4,1440]{2,1,0:T(4,128)S(1)}, u32[]{:S(2)}, u32[]{:S(2)}) %collective-permute-start.2) | collective-permute-done | bytes 92192 | tf_op jit(solution)/shard_map/ppermute | solution.py:282
  86.9 0.0 copy-done.1
  87.0 0.7 product_vertical.1
  87.6 31.6 %all_to_all.28 = f32[64,1,2944]{2,1,0:T(1,128)S(1)} all-to-all(f32[64,1,2944]{2,1,0:T(1,128)S(1)} %bitcast.15), channel_id=1, replica_groups=mesh['lat'=64,'y'=4,'core'=2] {'lat'}, dimensions={0} | all-to-all | bytes 1507328 | tf_op jit(solution)/shard_map/all_to_all | solution.py:264
  119.3 1.3 meridional.1
  120.6 5.7 %all-to-all-start.4 = ((f32[64,1,2944]{2,1,0:T(1,128)}), f32[64,1,2944]{2,1,0:T(1,128)S(1)}, u32[]{:S(2)}, u32[]{:S(2)}) async-start(f32[64,1,2944]{2,1,0:T(1,128)} %bitcast.10), calls=%async_computation.4 | async-start | bytes 1507328 | tf_op jit(solution)/shard_map/all_to_all | solution.py:264
  126.4 0.0 copy-start
  126.4 0.9 reach.1
  127.3 26.1 %all-to-all-done.4 = f32[64,1,2944]{2,1,0:T(1,128)S(1)} async-done(((f32[64,1,2944]{2,1,0:T(1,128)}), f32[64,1,2944]{2,1,0:T(1,128)S(1)}, u32[]{:S(2)}, u32[]{:S(2)}) %all-to-all-start.4) | async-done | bytes 753696 | tf_op jit(solution)/shard_map/all_to_all | solution.py:264
  153.4 0.0 copy-done
  153.4 2.9 %zonal.1 = f32[1440,128]{1,0:T(8,128)} custom-call(bf16[288,1440]{1,0:T(8,128)(2,1)S(1)} %get-tuple-element.7.high_ref, bf16[288,1440]{1,0:T(8,128)(2,1)S(1)} %get-tuple-element.8.low_ref, f32[1472,128]{1,0:T(8,128)S(1)} %bitcast.14, bf16[1440,128]{1,0:T(8,128)(2,1)S(1)} %bitcast.19), custom_call_target="tpu_custom_call" | custom-call | tf_op jit(solution)/shard_map/zonal/pallas_call | solution.py:248
  (3 shorter events, 0.1 us)
Async XLA Ops:
  57.4 29.6 %copy-start.1 = (bf16[1,1440,128]{2,1,0:T(8,128)(2,1)S(1)}, bf16[1,1440,128]{2,1,0:T(8,128)(2,1)}, u32[]{:S(2)}) copy-start(bf16[1,1440,128]{2,1,0:T(8,128)(2,1)} %param.10) | copy-start | bytes 1105924
  66.7 6.6 %collective-permute-start = (f32[4,4,1440]{2,1,0:T(4,128)S(1)}, f32[4,4,1440]{2,1,0:T(4,128)S(1)}, u32[]{:S(2)}, u32[]{:S(2)}) collective-permute-start(f32[4,4,1440]{2,1,0:T(4,128)S(1)} %slice.4), channel_id=1, source_target_pairs={{1,3},{3,5},{5,7},{7,1},{9,11},{11,13},{13,15},{15,9},{17,19},{19,... | collective-permute-start | bytes 276488 | tf_op jit(solution)/shard_map/ppermute | solution.py:282
  73.2 6.9 %collective-permute-start.1 = (f32[4,4,1440]{2,1,0:T(4,128)S(1)}, f32[4,4,1440]{2,1,0:T(4,128)S(1)}, u32[]{:S(2)}, u32[]{:S(2)}) collective-permute-start(f32[4,4,1440]{2,1,0:T(4,128)S(1)} %collective-permute-done), channel_id=1, source_target_pairs={{1,3},{3,5},{5,7},{7,1},{9,11},{11,13},{13,15},{15,9},{17,19},{19,... | collective-permute-start | bytes 276488 | tf_op jit(solution)/shard_map/ppermute | solution.py:282
  80.1 6.9 %collective-permute-start.2 = (f32[4,4,1440]{2,1,0:T(4,128)S(1)}, f32[4,4,1440]{2,1,0:T(4,128)S(1)}, u32[]{:S(2)}, u32[]{:S(2)}) collective-permute-start(f32[4,4,1440]{2,1,0:T(4,128)S(1)} %collective-permute-done.1), channel_id=1, source_target_pairs={{1,3},{3,5},{5,7},{7,1},{9,11},{11,13},{13,15},{15,9},{17,19},{19,... | collective-permute-start | bytes 276488 | tf_op jit(solution)/shard_map/ppermute | solution.py:282
  120.6 32.8 %all-to-all-start.4 = ((f32[64,1,2944]{2,1,0:T(1,128)}), f32[64,1,2944]{2,1,0:T(1,128)S(1)}, u32[]{:S(2)}, u32[]{:S(2)}) async-start(f32[64,1,2944]{2,1,0:T(1,128)} %bitcast.10), calls=%async_computation.4 | async-start | bytes 1507328 | tf_op jit(solution)/shard_map/all_to_all | solution.py:264
  126.4 27.0 %copy-start = (bf16[1,1440,128]{2,1,0:T(8,128)(2,1)S(1)}, bf16[1,1440,128]{2,1,0:T(8,128)(2,1)}, u32[]{:S(2)}) copy-start(bf16[1,1440,128]{2,1,0:T(8,128)(2,1)} %param.11) | copy-start | bytes 1105924

commit v6 on v5

--- a/solution.py
+++ b/solution.py
@@ -277,7 +277,7 @@
 
     rings = lax.axis_size("y")
     second = [(2 * y + 1, 2 * ((y + 1) % rings) + 1) for y in range(rings)]
-    turn = innovation[:4]
+    turn = innovation[:5]
     for _ in range(3):
         turn = lax.ppermute(turn, ("y", "core"), second)
     vertical = product_vertical(turn, perturb[0], innovation, padded)

time: 158 us -> 157 us (level)
  no operation moved by 1% of the time
where the time goes in v6:
time: 157 us
  blocking collectives  94.4 us (60%)
  waiting for transfers between devices  40.5 us (26%)
  starting transfers between devices  12 us (8%)
  Pallas kernels  9.51 us (6%)
    all_to_all x4, blocking collectives, exchange(): return lax.all_to_all(pieces, axes, split_axis=0, concat_axis=0, tiled=True)  94.4 us
    all_to_all x1, waiting for transfers between devices, exchange(): return lax.all_to_all(pieces, axes, split_axis=0, concat_axis=0, tiled=True)  25.8 us
    ppermute x3, waiting for transfers between devices, local(): turn = lax.ppermute(turn, ('y', 'core'), second)  14.7 us
    ppermute x3, starting transfers between devices, local(): turn = lax.ppermute(turn, ('y', 'core'), second)  6.3 us
    all_to_all x1, starting transfers between devices, exchange(): return lax.all_to_all(pieces, axes, split_axis=0, concat_axis=0, tiled=True)  5.71 us
  transfers between devices with their start and end apart: 4, of which 4 were waited for; matrix products, arithmetic and copies ran while one was open for 0% of the time, Pallas kernels for 1%

profile of v6, /device:TPU:1, one launch (start us, length us, event | category | flops | bytes accessed | tf_op | source)
XLA Modules:
  0.0 156.7 jit_solution(14553044730415768349)
XLA Ops:
  0.0 2.3 %bucket.1 = f32[576,128]{1,0:T(8,128)S(1)} custom-call(f32[32,512]{1,0:T(8,128)} %bitcast.21, s32[1,512]{1,0:T(1,128)} %bitcast.22, s32[1,512]{1,0:T(1,128)} %bitcast.23, s32[1,512]{1,0:T(1,128)} %bitcast.24), custom_call_target="tpu_custom_call" | custom-call | tf_op jit(solution)/shard_map/bucket/pallas_call | solution.py:86
  2.3 39.4 %all_to_all.25 = f32[64,1,1152]{2,1,0:T(1,128)S(1)} all-to-all(f32[64,1,1152]{2,1,0:T(1,128)S(1)} %bitcast.17), channel_id=1, replica_groups=mesh['lat'=64,'y'=4,'core'=2] {'lat'}, dimensions={0} | all-to-all | bytes 589824 | tf_op jit(solution)/shard_map/all_to_all | solution.py:264
  41.7 1.5 deposit.1
  43.2 14.2 %all_to_all.26 = f32[8,4,1440]{2,1,0:T(4,128)S(1)} all-to-all(f32[8,4,1440]{2,1,0:T(4,128)S(1)} %deposit.1), channel_id=1, replica_groups=mesh['lat'=64,'y'=4,'core'=2] {'core','y'}, dimensions={0} | all-to-all | bytes 368640 | tf_op jit(solution)/shard_map/all_to_all | solution.py:264
  57.4 0.0 copy-start.1
  57.4 9.2 %all_to_all.27.innovation_ref = f32[8,4,1440]{2,1,0:T(4,128)S(1)} all-to-all(f32[8,4,1440]{2,1,0:T(4,128)S(1)} %broadcast_in_dim.4), channel_id=1, replica_groups=mesh['lat'=64,'y'=4,'core'=2] {'core','y'}, dimensions={0} | all-to-all | bytes 368640 | tf_op jit(solution)/shard_map/all_to_all | solution.py:264
  66.7 2.5 %collective-permute-start = (f32[5,4,1440]{2,1,0:T(4,128)S(1)}, f32[5,4,1440]{2,1,0:T(4,128)S(1)}, u32[]{:S(2)}, u32[]{:S(2)}) collective-permute-start(f32[5,4,1440]{2,1,0:T(4,128)S(1)} %slice.4), channel_id=1, source_target_pairs={{1,3},{3,5},{5,7},{7,1},{9,11},{11,13},{13,15},{15,9},{17,19},{19,... | collective-permute-start | bytes 345608 | tf_op jit(solution)/shard_map/ppermute | solution.py:282
  69.2 4.3 %collective-permute-done = f32[5,4,1440]{2,1,0:T(4,128)S(1)} collective-permute-done((f32[5,4,1440]{2,1,0:T(4,128)S(1)}, f32[5,4,1440]{2,1,0:T(4,128)S(1)}, u32[]{:S(2)}, u32[]{:S(2)}) %collective-permute-start) | collective-permute-done | bytes 115232 | tf_op jit(solution)/shard_map/ppermute | solution.py:282
  73.5 1.9 %collective-permute-start.1 = (f32[5,4,1440]{2,1,0:T(4,128)S(1)}, f32[5,4,1440]{2,1,0:T(4,128)S(1)}, u32[]{:S(2)}, u32[]{:S(2)}) collective-permute-start(f32[5,4,1440]{2,1,0:T(4,128)S(1)} %collective-permute-done), channel_id=1, source_target_pairs={{1,3},{3,5},{5,7},{7,1},{9,11},{11,13},{13,15},{15,9},{17,19},{19,... | collective-permute-start | bytes 345608 | tf_op jit(solution)/shard_map/ppermute | solution.py:282
  75.4 5.2 %collective-permute-done.1 = f32[5,4,1440]{2,1,0:T(4,128)S(1)} collective-permute-done((f32[5,4,1440]{2,1,0:T(4,128)S(1)}, f32[5,4,1440]{2,1,0:T(4,128)S(1)}, u32[]{:S(2)}, u32[]{:S(2)}) %collective-permute-start.1) | collective-permute-done | bytes 115232 | tf_op jit(solution)/shard_map/ppermute | solution.py:282
  80.6 1.9 %collective-permute-start.2 = (f32[5,4,1440]{2,1,0:T(4,128)S(1)}, f32[5,4,1440]{2,1,0:T(4,128)S(1)}, u32[]{:S(2)}, u32[]{:S(2)}) collective-permute-start(f32[5,4,1440]{2,1,0:T(4,128)S(1)} %collective-permute-done.1), channel_id=1, source_target_pairs={{1,3},{3,5},{5,7},{7,1},{9,11},{11,13},{13,15},{15,9},{17,19},{19,... | collective-permute-start | bytes 345608 | tf_op jit(solution)/shard_map/ppermute | solution.py:282
  82.5 5.2 %collective-permute-done.2.turn_ref = f32[5,4,1440]{2,1,0:T(4,128)S(1)} collective-permute-done((f32[5,4,1440]{2,1,0:T(4,128)S(1)}, f32[5,4,1440]{2,1,0:T(4,128)S(1)}, u32[]{:S(2)}, u32[]{:S(2)}) %collective-permute-start.2) | collective-permute-done | bytes 115232 | tf_op jit(solution)/shard_map/ppermute | solution.py:282
  87.7 0.0 copy-done.1
  87.7 0.7 product_vertical.1
  88.4 31.6 %all_to_all.28 = f32[64,1,2944]{2,1,0:T(1,128)S(1)} all-to-all(f32[64,1,2944]{2,1,0:T(1,128)S(1)} %bitcast.15), channel_id=1, replica_groups=mesh['lat'=64,'y'=4,'core'=2] {'lat'}, dimensions={0} | all-to-all | bytes 1507328 | tf_op jit(solution)/shard_map/all_to_all | solution.py:264
  120.1 1.3 meridional.1
  121.3 5.7 %all-to-all-start.4 = ((f32[64,1,2944]{2,1,0:T(1,128)}), f32[64,1,2944]{2,1,0:T(1,128)S(1)}, u32[]{:S(2)}, u32[]{:S(2)}) async-start(f32[64,1,2944]{2,1,0:T(1,128)} %bitcast.10), calls=%async_computation.4 | async-start | bytes 1507328 | tf_op jit(solution)/shard_map/all_to_all | solution.py:264
  127.2 0.0 copy-start
  127.2 0.9 reach.1
  128.1 25.8 %all-to-all-done.4 = f32[64,1,2944]{2,1,0:T(1,128)S(1)} async-done(((f32[64,1,2944]{2,1,0:T(1,128)}), f32[64,1,2944]{2,1,0:T(1,128)S(1)}, u32[]{:S(2)}, u32[]{:S(2)}) %all-to-all-start.4) | async-done | bytes 753696 | tf_op jit(solution)/shard_map/all_to_all | solution.py:264
  153.8 0.0 copy-done
  153.8 2.9 %zonal.1 = f32[1440,128]{1,0:T(8,128)} custom-call(bf16[288,1440]{1,0:T(8,128)(2,1)S(1)} %get-tuple-element.7.high_ref, bf16[288,1440]{1,0:T(8,128)(2,1)S(1)} %get-tuple-element.8.low_ref, f32[1472,128]{1,0:T(8,128)S(1)} %bitcast.14, bf16[1440,128]{1,0:T(8,128)(2,1)S(1)} %bitcast.19), custom_call_target="tpu_custom_call" | custom-call | tf_op jit(solution)/shard_map/zonal/pallas_call | solution.py:248
  (3 shorter events, 0.1 us)
Async XLA Ops:
  57.4 30.3 %copy-start.1 = (bf16[1,1440,128]{2,1,0:T(8,128)(2,1)S(1)}, bf16[1,1440,128]{2,1,0:T(8,128)(2,1)}, u32[]{:S(2)}) copy-start(bf16[1,1440,128]{2,1,0:T(8,128)(2,1)} %param.10) | copy-start | bytes 1105924
  66.7 6.8 %collective-permute-start = (f32[5,4,1440]{2,1,0:T(4,128)S(1)}, f32[5,4,1440]{2,1,0:T(4,128)S(1)}, u32[]{:S(2)}, u32[]{:S(2)}) collective-permute-start(f32[5,4,1440]{2,1,0:T(4,128)S(1)} %slice.4), channel_id=1, source_target_pairs={{1,3},{3,5},{5,7},{7,1},{9,11},{11,13},{13,15},{15,9},{17,19},{19,... | collective-permute-start | bytes 345608 | tf_op jit(solution)/shard_map/ppermute | solution.py:282
  73.5 7.1 %collective-permute-start.1 = (f32[5,4,1440]{2,1,0:T(4,128)S(1)}, f32[5,4,1440]{2,1,0:T(4,128)S(1)}, u32[]{:S(2)}, u32[]{:S(2)}) collective-permute-start(f32[5,4,1440]{2,1,0:T(4,128)S(1)} %collective-permute-done), channel_id=1, source_target_pairs={{1,3},{3,5},{5,7},{7,1},{9,11},{11,13},{13,15},{15,9},{17,19},{19,... | collective-permute-start | bytes 345608 | tf_op jit(solution)/shard_map/ppermute | solution.py:282
  80.6 7.1 %collective-permute-start.2 = (f32[5,4,1440]{2,1,0:T(4,128)S(1)}, f32[5,4,1440]{2,1,0:T(4,128)S(1)}, u32[]{:S(2)}, u32[]{:S(2)}) collective-permute-start(f32[5,4,1440]{2,1,0:T(4,128)S(1)} %collective-permute-done.1), channel_id=1, source_target_pairs={{1,3},{3,5},{5,7},{7,1},{9,11},{11,13},{13,15},{15,9},{17,19},{19,... | collective-permute-start | bytes 345608 | tf_op jit(solution)/shard_map/ppermute | solution.py:282
  121.3 32.5 %all-to-all-start.4 = ((f32[64,1,2944]{2,1,0:T(1,128)}), f32[64,1,2944]{2,1,0:T(1,128)S(1)}, u32[]{:S(2)}, u32[]{:S(2)}) async-start(f32[64,1,2944]{2,1,0:T(1,128)} %bitcast.10), calls=%async_computation.4 | async-start | bytes 1507328 | tf_op jit(solution)/shard_map/all_to_all | solution.py:264
  127.2 26.6 %copy-start = (bf16[1,1440,128]{2,1,0:T(8,128)(2,1)S(1)}, bf16[1,1440,128]{2,1,0:T(8,128)(2,1)}, u32[]{:S(2)}) copy-start(bf16[1,1440,128]{2,1,0:T(8,128)(2,1)} %param.11) | copy-start | bytes 1105924

commit v7 on v6

--- a/solution.py
+++ b/solution.py
@@ -277,7 +277,7 @@
 
     rings = lax.axis_size("y")
     second = [(2 * y + 1, 2 * ((y + 1) % rings) + 1) for y in range(rings)]
-    turn = innovation[:5]
+    turn = innovation[:6]
     for _ in range(3):
         turn = lax.ppermute(turn, ("y", "core"), second)
     vertical = product_vertical(turn, perturb[0], innovation, padded)

time: 157 us -> 158 us (level)
  no operation moved by 1% of the time
where the time goes in v7:
time: 158 us
  blocking collectives  94.4 us (60%)
  waiting for transfers between devices  41.3 us (26%)
  starting transfers between devices  12.1 us (8%)
  Pallas kernels  9.51 us (6%)
    all_to_all x4, blocking collectives, exchange(): return lax.all_to_all(pieces, axes, split_axis=0, concat_axis=0, tiled=True)  94.4 us
    all_to_all x1, waiting for transfers between devices, exchange(): return lax.all_to_all(pieces, axes, split_axis=0, concat_axis=0, tiled=True)  25.8 us
    ppermute x3, waiting for transfers between devices, local(): turn = lax.ppermute(turn, ('y', 'core'), second)  15.5 us
    ppermute x3, starting transfers between devices, local(): turn = lax.ppermute(turn, ('y', 'core'), second)  6.3 us
    all_to_all x1, starting transfers between devices, exchange(): return lax.all_to_all(pieces, axes, split_axis=0, concat_axis=0, tiled=True)  5.84 us
  transfers between devices with their start and end apart: 4, of which 4 were waited for; matrix products, arithmetic and copies ran while one was open for 0% of the time, Pallas kernels for 1%

profile of v7, /device:TPU:1, one launch (start us, length us, event | category | flops | bytes accessed | tf_op | source)
XLA Modules:
  0.0 157.6 jit_solution(10590111830382939538)
XLA Ops:
  0.0 2.3 %bucket.1 = f32[576,128]{1,0:T(8,128)S(1)} custom-call(f32[32,512]{1,0:T(8,128)} %bitcast.21, s32[1,512]{1,0:T(1,128)} %bitcast.22, s32[1,512]{1,0:T(1,128)} %bitcast.23, s32[1,512]{1,0:T(1,128)} %bitcast.24), custom_call_target="tpu_custom_call" | custom-call | tf_op jit(solution)/shard_map/bucket/pallas_call | solution.py:86
  2.3 39.4 %all_to_all.25 = f32[64,1,1152]{2,1,0:T(1,128)S(1)} all-to-all(f32[64,1,1152]{2,1,0:T(1,128)S(1)} %bitcast.17), channel_id=1, replica_groups=mesh['lat'=64,'y'=4,'core'=2] {'lat'}, dimensions={0} | all-to-all | bytes 589824 | tf_op jit(solution)/shard_map/all_to_all | solution.py:264
  41.7 1.5 deposit.1
  43.2 14.2 %all_to_all.26 = f32[8,4,1440]{2,1,0:T(4,128)S(1)} all-to-all(f32[8,4,1440]{2,1,0:T(4,128)S(1)} %deposit.1), channel_id=1, replica_groups=mesh['lat'=64,'y'=4,'core'=2] {'core','y'}, dimensions={0} | all-to-all | bytes 368640 | tf_op jit(solution)/shard_map/all_to_all | solution.py:264
  57.4 0.0 copy-start.1
  57.4 9.2 %all_to_all.27.innovation_ref = f32[8,4,1440]{2,1,0:T(4,128)S(1)} all-to-all(f32[8,4,1440]{2,1,0:T(4,128)S(1)} %broadcast_in_dim.4), channel_id=1, replica_groups=mesh['lat'=64,'y'=4,'core'=2] {'core','y'}, dimensions={0} | all-to-all | bytes 368640 | tf_op jit(solution)/shard_map/all_to_all | solution.py:264
  66.7 2.5 %collective-permute-start = (f32[6,4,1440]{2,1,0:T(4,128)S(1)}, f32[6,4,1440]{2,1,0:T(4,128)S(1)}, u32[]{:S(2)}, u32[]{:S(2)}) collective-permute-start(f32[6,4,1440]{2,1,0:T(4,128)S(1)} %slice.4), channel_id=1, source_target_pairs={{1,3},{3,5},{5,7},{7,1},{9,11},{11,13},{13,15},{15,9},{17,19},{19,... | collective-permute-start | bytes 414728 | tf_op jit(solution)/shard_map/ppermute | solution.py:282
  69.2 4.6 %collective-permute-done = f32[6,4,1440]{2,1,0:T(4,128)S(1)} collective-permute-done((f32[6,4,1440]{2,1,0:T(4,128)S(1)}, f32[6,4,1440]{2,1,0:T(4,128)S(1)}, u32[]{:S(2)}, u32[]{:S(2)}) %collective-permute-start) | collective-permute-done | bytes 138272 | tf_op jit(solution)/shard_map/ppermute | solution.py:282
  73.8 1.9 %collective-permute-start.1 = (f32[6,4,1440]{2,1,0:T(4,128)S(1)}, f32[6,4,1440]{2,1,0:T(4,128)S(1)}, u32[]{:S(2)}, u32[]{:S(2)}) collective-permute-start(f32[6,4,1440]{2,1,0:T(4,128)S(1)} %collective-permute-done), channel_id=1, source_target_pairs={{1,3},{3,5},{5,7},{7,1},{9,11},{11,13},{13,15},{15,9},{17,19},{19,... | collective-permute-start | bytes 414728 | tf_op jit(solution)/shard_map/ppermute | solution.py:282
  75.7 5.5 %collective-permute-done.1 = f32[6,4,1440]{2,1,0:T(4,128)S(1)} collective-permute-done((f32[6,4,1440]{2,1,0:T(4,128)S(1)}, f32[6,4,1440]{2,1,0:T(4,128)S(1)}, u32[]{:S(2)}, u32[]{:S(2)}) %collective-permute-start.1) | collective-permute-done | bytes 138272 | tf_op jit(solution)/shard_map/ppermute | solution.py:282
  81.2 1.9 %collective-permute-start.2 = (f32[6,4,1440]{2,1,0:T(4,128)S(1)}, f32[6,4,1440]{2,1,0:T(4,128)S(1)}, u32[]{:S(2)}, u32[]{:S(2)}) collective-permute-start(f32[6,4,1440]{2,1,0:T(4,128)S(1)} %collective-permute-done.1), channel_id=1, source_target_pairs={{1,3},{3,5},{5,7},{7,1},{9,11},{11,13},{13,15},{15,9},{17,19},{19,... | collective-permute-start | bytes 414728 | tf_op jit(solution)/shard_map/ppermute | solution.py:282
  83.1 5.5 %collective-permute-done.2.turn_ref = f32[6,4,1440]{2,1,0:T(4,128)S(1)} collective-permute-done((f32[6,4,1440]{2,1,0:T(4,128)S(1)}, f32[6,4,1440]{2,1,0:T(4,128)S(1)}, u32[]{:S(2)}, u32[]{:S(2)}) %collective-permute-start.2) | collective-permute-done | bytes 138272 | tf_op jit(solution)/shard_map/ppermute | solution.py:282
  88.5 0.0 copy-done.1
  88.5 0.7 product_vertical.1
  89.2 31.6 %all_to_all.28 = f32[64,1,2944]{2,1,0:T(1,128)S(1)} all-to-all(f32[64,1,2944]{2,1,0:T(1,128)S(1)} %bitcast.15), channel_id=1, replica_groups=mesh['lat'=64,'y'=4,'core'=2] {'lat'}, dimensions={0} | all-to-all | bytes 1507328 | tf_op jit(solution)/shard_map/all_to_all | solution.py:264
  120.9 1.3 meridional.1
  122.1 5.8 %all-to-all-start.4 = ((f32[64,1,2944]{2,1,0:T(1,128)}), f32[64,1,2944]{2,1,0:T(1,128)S(1)}, u32[]{:S(2)}, u32[]{:S(2)}) async-start(f32[64,1,2944]{2,1,0:T(1,128)} %bitcast.10), calls=%async_computation.4 | async-start | bytes 1507328 | tf_op jit(solution)/shard_map/all_to_all | solution.py:264
  128.1 0.0 copy-start
  128.1 0.9 reach.1
  129.0 25.8 %all-to-all-done.4 = f32[64,1,2944]{2,1,0:T(1,128)S(1)} async-done(((f32[64,1,2944]{2,1,0:T(1,128)}), f32[64,1,2944]{2,1,0:T(1,128)S(1)}, u32[]{:S(2)}, u32[]{:S(2)}) %all-to-all-start.4) | async-done | bytes 753696 | tf_op jit(solution)/shard_map/all_to_all | solution.py:264
  154.7 0.0 copy-done
  154.7 2.9 %zonal.1 = f32[1440,128]{1,0:T(8,128)} custom-call(bf16[288,1440]{1,0:T(8,128)(2,1)S(1)} %get-tuple-element.7.high_ref, bf16[288,1440]{1,0:T(8,128)(2,1)S(1)} %get-tuple-element.8.low_ref, f32[1472,128]{1,0:T(8,128)S(1)} %bitcast.14, bf16[1440,128]{1,0:T(8,128)(2,1)S(1)} %bitcast.19), custom_call_target="tpu_custom_call" | custom-call | tf_op jit(solution)/shard_map/zonal/pallas_call | solution.py:248
  (3 shorter events, 0.1 us)
Async XLA Ops:
  57.4 31.1 %copy-start.1 = (bf16[1,1440,128]{2,1,0:T(8,128)(2,1)S(1)}, bf16[1,1440,128]{2,1,0:T(8,128)(2,1)}, u32[]{:S(2)}) copy-start(bf16[1,1440,128]{2,1,0:T(8,128)(2,1)} %param.10) | copy-start | bytes 1105924
  66.7 7.1 %collective-permute-start = (f32[6,4,1440]{2,1,0:T(4,128)S(1)}, f32[6,4,1440]{2,1,0:T(4,128)S(1)}, u32[]{:S(2)}, u32[]{:S(2)}) collective-permute-start(f32[6,4,1440]{2,1,0:T(4,128)S(1)} %slice.4), channel_id=1, source_target_pairs={{1,3},{3,5},{5,7},{7,1},{9,11},{11,13},{13,15},{15,9},{17,19},{19,... | collective-permute-start | bytes 414728 | tf_op jit(solution)/shard_map/ppermute | solution.py:282
  73.8 7.4 %collective-permute-start.1 = (f32[6,4,1440]{2,1,0:T(4,128)S(1)}, f32[6,4,1440]{2,1,0:T(4,128)S(1)}, u32[]{:S(2)}, u32[]{:S(2)}) collective-permute-start(f32[6,4,1440]{2,1,0:T(4,128)S(1)} %collective-permute-done), channel_id=1, source_target_pairs={{1,3},{3,5},{5,7},{7,1},{9,11},{11,13},{13,15},{15,9},{17,19},{19,... | collective-permute-start | bytes 414728 | tf_op jit(solution)/shard_map/ppermute | solution.py:282
  81.2 7.4 %collective-permute-start.2 = (f32[6,4,1440]{2,1,0:T(4,128)S(1)}, f32[6,4,1440]{2,1,0:T(4,128)S(1)}, u32[]{:S(2)}, u32[]{:S(2)}) collective-permute-start(f32[6,4,1440]{2,1,0:T(4,128)S(1)} %collective-permute-done.1), channel_id=1, source_target_pairs={{1,3},{3,5},{5,7},{7,1},{9,11},{11,13},{13,15},{15,9},{17,19},{19,... | collective-permute-start | bytes 414728 | tf_op jit(solution)/shard_map/ppermute | solution.py:282
  122.1 32.6 %all-to-all-start.4 = ((f32[64,1,2944]{2,1,0:T(1,128)}), f32[64,1,2944]{2,1,0:T(1,128)S(1)}, u32[]{:S(2)}, u32[]{:S(2)}) async-start(f32[64,1,2944]{2,1,0:T(1,128)} %bitcast.10), calls=%async_computation.4 | async-start | bytes 1507328 | tf_op jit(solution)/shard_map/all_to_all | solution.py:264
  128.1 26.6 %copy-start = (bf16[1,1440,128]{2,1,0:T(8,128)(2,1)S(1)}, bf16[1,1440,128]{2,1,0:T(8,128)(2,1)}, u32[]{:S(2)}) copy-start(bf16[1,1440,128]{2,1,0:T(8,128)(2,1)} %param.11) | copy-start | bytes 1105924
